TPU v7x, 32 devices: a whole 2x2x4 slice. The times are simulated.
32 devices in a mesh: layer: 4 (over y, core), row: 8 (over z, x).
Axes of the slice: x: 2, y: 2, z: 4, core: 2. Of those that a mesh axis runs over, the one named last changes fastest.
Arguments:
- transmission: bfloat16 [4, 6144, 6144], P('layer', 'row'), may hold values from -0.078125 to 0.078125
- reflection: bfloat16 [4, 6144, 6144], P('layer', 'row'), may hold values from -0.078125 to 0.078125
- receiver_map: bfloat16 [4, 6144, 6144], P('layer', 'row'), may hold values from -0.078125 to 0.078125
- midplane_map: bfloat16 [4, 6144, 6144], P('layer', 'row'), may hold values from -0.078125 to 0.078125
- traces: bfloat16 [4, 6144, 384], P('layer', 'row'), may hold values from -6 to 6
- sources: bfloat16 [4, 3, 6144, 384], P('layer', None, 'row'), may hold values from -5 to 5
Outputs:
- reflected: bfloat16 [4, 3, 6144, 384], P('layer', None, 'row')
- recorded: bfloat16 [4, 3, 6144, 384], P('layer', None, 'row')
- midfield: bfloat16 [4, 3, 6144, 384], P('layer', None, 'row')
- transmitted: bfloat16 [4, 6144, 384], P('layer', 'row')
All inputs are finite; a program needn't handle non-finite values.
Results may differ from a plain program's by a relative error of at most 0.0052.
Values may be sent and summed in bfloat16 or wider, within the bound.
No kernel may reach another device: no remote copies, remote signals or barrier semaphores. Data moves between devices by JAX's collectives and lax.ppermute only.
A program may use at most 128 MiB of HBM per device.

v0:
```python
import jax
import jax.numpy as jnp
from jax import lax
from jax.sharding import PartitionSpec as P

TICKS = 3


def from_behind(x, axis, by):
    length = lax.axis_size(axis)
    pairs = [(i, i + by) for i in range(length) if 0 <= i + by < length]
    return lax.ppermute(x, axis, pairs)


def pass_down(sent):
    return from_behind(sent, "layer", 1)


def shards(transmission, reflection, receiver_map, midplane_map, traces, sources):
    transmit_rows = transmission[0]
    reflect_rows = reflection[0]
    receive_rows = receiver_map[0]
    middle_rows = midplane_map[0]
    incoming = traces[0]
    bounced_all = []
    heard_all = []
    middle_all = []
    sent = incoming
    for tick in range(TICKS):
        source_now = sources[0, tick].astype(jnp.float32)
        piece = lax.all_gather(incoming, "row", axis=0, tiled=True)
        results = []
        for index, matrix in enumerate((transmit_rows, reflect_rows, receive_rows, middle_rows)):
            results.append(jnp.dot(matrix, piece, preferred_element_type=jnp.float32))
        trans_sum = results[0]
        reflect_sum = results[1]
        heard_sum = results[2]
        middle_sum = results[3]
        sent = (trans_sum + source_now).astype(jnp.bfloat16)
        if tick + 1 < TICKS:
            incoming = pass_down(sent)
        bounced_all.append(reflect_sum.astype(jnp.bfloat16))
        heard_all.append(heard_sum.astype(jnp.bfloat16))
        middle_all.append(middle_sum.astype(jnp.bfloat16))
    return (
        jnp.stack(bounced_all, axis=0)[None],
        jnp.stack(heard_all, axis=0)[None],
        jnp.stack(middle_all, axis=0)[None],
        sent[None],
    )


def solution(mesh):
    return jax.shard_map(
        shards,
        mesh=mesh,
        in_specs=(
            P("layer", "row", None),
            P("layer", "row", None),
            P("layer", "row", None),
            P("layer", "row", None),
            P("layer", "row", None),
            P("layer", None, "row", None),
        ),
        out_specs=(
            P("layer", None, "row", None),
            P("layer", None, "row", None),
            P("layer", None, "row", None),
            P("layer", "row", None),
        ),
        check_vma=False,
    )
```

profile of v0, /device:TPU:0, one launch (start us, length us, event | category | flops | bytes accessed | tf_op | source)
XLA Modules:
  0.0 336.2 jit_solution(7303743776478562701)
XLA Ops:
  8.0 84.3 %all-gather.9.cloned.1.call-done = bf16[1,6144,384]{2,1,0:T(8,128)(2,1)} async-done(((bf16[1,768,384]{2,1,0:T(8,128)(2,1)}), bf16[1,6144,384]{2,1,0:T(8,128)(2,1)}) %all-gather.9.cloned.1.call-update) | async-done | bytes 4718608 | tf_op jit(solution)/shard_map/all_gather | solution.py:31
  92.2 9.2 %fusion.45 = bf16[768,384]{1,0:T(8,128)(2,1)S(1)} fusion(bf16[1,6144,384]{2,1,0:T(8,128)(2,1)} %all-gather.9.cloned.1.call-done, bf16[1,768,6144]{2,1,0:T(8,128)(2,1)} %param.6, bf16[1,3,768,384]{3,2,1,0:T(8,128)(2,1)} %param.11), kind=kOutput, calls=%fused_computation.36 | convolution fusion | flops 3624763392 | bytes 15335424 | tf_op jit(solution)/shard_map/dot_general | solution.py:34
  101.4 1.3 collective-permute-start
  102.7 1.6 collective-permute-done
  105.6 85.7 %all-gather.5.cloned.1.call-done = bf16[6144,384]{1,0:T(8,128)(2,1)} async-done(((bf16[768,384]{1,0:T(8,128)(2,1)}), bf16[6144,384]{1,0:T(8,128)(2,1)}) %all-gather.5.cloned.1.call-update) | async-done | bytes 4718608 | tf_op jit(solution)/shard_map/all_gather | solution.py:31
  191.3 9.0 %fusion.50 = bf16[768,384]{0,1:T(8,128)(2,1)S(1)} fusion(bf16[6144,384]{1,0:T(8,128)(2,1)} %all-gather.5.cloned.1.call-done, bf16[1,768,6144]{2,1,0:T(8,128)(2,1)} %param.6, bf16[1,1,768,384]{2,3,1,0:T(8,128)(2,1)S(1)} %copy.25), kind=kOutput, calls=%fused_computation.37 | convolution fusion | flops 3624763392 | bytes 15335424 | tf_op jit(solution)/shard_map/dot_general | solution.py:34
  200.3 1.3 collective-permute-start.1
  201.6 1.6 collective-permute-done.1
  203.2 0.8 copy-done.1
  204.0 1.1 copy.26
  205.1 9.1 %fusion.112 = bf16[1,768,384]{2,1,0:T(8,128)(2,1)S(1)} fusion(bf16[1,6144,384]{2,1,0:T(8,128)(2,1)} %all-gather.9.cloned.1.call-done, bf16[1,768,6144]{2,1,0:T(8,128)(2,1)} %param.8), kind=kOutput, calls=%fused_computation.55 | convolution fusion | flops 3624173568 | bytes 14745600 | tf_op jit(solution)/shard_map/dot_general | solution.py:34
  214.3 9.4 %fusion.107 = bf16[1,768,384]{2,1,0:T(8,128)(2,1)S(1)} fusion(bf16[1,6144,384]{2,1,0:T(8,128)(2,1)} %all-gather.9.cloned.1.call-done, bf16[1,768,6144]{2,1,0:T(8,128)(2,1)} %param.9), kind=kOutput, calls=%fused_computation.54 | convolution fusion | flops 3624173568 | bytes 14745600 | tf_op jit(solution)/shard_map/dot_general | solution.py:34
  223.7 5.0 %fusion.117 = bf16[1,768,384]{2,1,0:T(8,128)(2,1)S(1)} fusion(bf16[1,6144,384]{2,1,0:T(8,128)(2,1)S(1)} %bitcast.185, bf16[1,768,6144]{2,1,0:T(8,128)(2,1)S(1)} %bitcast.181), kind=kOutput, calls=%fused_computation.56 | convolution fusion | flops 3624173568 | bytes 14745600 | tf_op jit(solution)/shard_map/dot_general | solution.py:34
  228.8 7.5 %fusion.104 = bf16[1,768,384]{2,1,0:T(8,128)(2,1)S(1)} fusion(bf16[6144,384]{1,0:T(8,128)(2,1)} %all-gather.5.cloned.1.call-done, bf16[1,768,6144]{2,1,0:T(8,128)(2,1)S(1)} %bitcast.181), kind=kOutput, calls=%fused_computation.53 | convolution fusion | flops 3624173568 | bytes 14745600 | tf_op jit(solution)/shard_map/dot_general | solution.py:34
  236.4 5.0 %fusion.98 = bf16[1,768,384]{2,1,0:T(8,128)(2,1)S(1)} fusion(bf16[6144,384]{1,0:T(8,128)(2,1)S(1)} %bitcast.187, bf16[1,768,6144]{2,1,0:T(8,128)(2,1)S(1)} %bitcast.179), kind=kOutput, calls=%fused_computation.51 | convolution fusion | flops 3624173568 | bytes 14745600 | tf_op jit(solution)/shard_map/dot_general | solution.py:34
  241.5 5.3 %fusion.92 = bf16[1,768,384]{2,1,0:T(8,128)(2,1)S(1)} fusion(bf16[6144,384]{1,0:T(8,128)(2,1)S(1)} %bitcast.187, bf16[1,768,6144]{2,1,0:T(8,128)(2,1)S(1)} %bitcast.177), kind=kOutput, calls=%fused_computation.49 | convolution fusion | flops 3624173568 | bytes 14745600 | tf_op jit(solution)/shard_map/dot_general | solution.py:34
  246.7 43.2 %all-gather.7.cloned.1.call-done = bf16[6144,384]{0,1:T(8,128)(2,1)} async-done(((bf16[768,384]{0,1:T(8,128)(2,1)}), bf16[6144,384]{0,1:T(8,128)(2,1)}) %all-gather.7.cloned.1.call-update) | async-done | bytes 4718608 | tf_op jit(solution)/shard_map/all_gather | solution.py:31
  289.9 9.8 %fusion.122 = bf16[1,768,384]{1,2,0:T(8,128)(2,1)} fusion(bf16[6144,384]{0,1:T(8,128)(2,1)} %all-gather.7.cloned.1.call-done, bf16[1,768,6144]{2,1,0:T(8,128)(2,1)} %param.6, bf16[1,1,768,384]{2,3,1,0:T(8,128)(2,1)} %copy.26), kind=kOutput, calls=%fused_computation.57 | convolution fusion | flops 3624763392 | bytes 15335424 | tf_op jit(solution)/shard_map/dot_general | solution.py:34
  299.7 2.1 copy.18
  301.8 9.0 %fusion.89 = bf16[1,768,384]{2,1,0:T(8,128)(2,1)S(1)} fusion(bf16[6144,384]{0,1:T(8,128)(2,1)} %all-gather.7.cloned.1.call-done, bf16[1,768,6144]{2,1,0:T(8,128)(2,1)} %param.9), kind=kOutput, calls=%fused_computation.48 | convolution fusion | flops 3624173568 | bytes 14745600 | tf_op jit(solution)/shard_map/dot_general | solution.py:34
  310.8 1.4 maximum_bitcast_fusion.2
  312.3 10.2 %fusion.95 = bf16[1,768,384]{2,1,0:T(8,128)(2,1)S(1)} fusion(bf16[6144,384]{0,1:T(8,128)(2,1)} %all-gather.7.cloned.1.call-done, bf16[1,768,6144]{2,1,0:T(8,128)(2,1)} %param.8), kind=kOutput, calls=%fused_computation.50 | convolution fusion | flops 3624173568 | bytes 14745600 | tf_op jit(solution)/shard_map/dot_general | solution.py:34
  322.5 5.0 %fusion.101 = bf16[1,768,384]{2,1,0:T(8,128)(2,1)S(1)} fusion(bf16[6144,384]{0,1:T(8,128)(2,1)S(1)} %bitcast.189, bf16[1,768,6144]{2,1,0:T(8,128)(2,1)S(1)} %bitcast.183), kind=kOutput, calls=%fused_computation.52 | convolution fusion | flops 3624173568 | bytes 14745600 | tf_op jit(solution)/shard_map/dot_general | solution.py:34
  327.6 2.1 maximum_bitcast_fusion
  (56 shorter events, 2.1 us)
Async XLA Ops:
  7.2 85.1 %all-gather.9.cloned.1.call-start = ((), (), s32[]{:S(2)}) async-start(), calls=%async_computation.2 | async-start | bytes 5308416 | tf_op jit(solution)/shard_map/all_gather | solution.py:31
  7.9 97.3 %copy-start = (bf16[1,3,768,384]{3,2,1,0:T(8,128)(2,1)S(1)}, bf16[1,3,768,384]{3,2,1,0:T(8,128)(2,1)}, u32[]{:S(2)}) copy-start(bf16[1,3,768,384]{3,2,1,0:T(8,128)(2,1)} %param.11) | copy-start | bytes 5308420
  7.9 183.4 %all-gather.5.cloned.1.call-start = ((), (), s32[]{:S(2)}) async-start(), calls=%async_computation | async-start | bytes 5308416 | tf_op jit(solution)/shard_map/all_gather | solution.py:31
  101.4 2.9 collective-permute-start
  105.1 184.7 %all-gather.7.cloned.1.call-start = ((), (), s32[]{:S(2)}) async-start(), calls=%async_computation.1 | async-start | bytes 5308416 | tf_op jit(solution)/shard_map/all_gather | solution.py:31
  200.3 2.9 collective-permute-start.1
  205.1 18.5 %slice-start.6 = ((s8[9437184]{0:T(1024)(128)(4,1)}), s8[4194304]{0:T(1024)(128)(4,1)S(1)}, s32[]{:S(2)}) async-start(s8[9437184]{0:T(1024)(128)(4,1)} %bitcast.180), calls=%async_computation.9 | async-start | bytes 8388608
  205.1 18.5 %slice-start.7 = ((s8[9437184]{0:T(1024)(128)(4,1)}), s8[4194304]{0:T(1024)(128)(4,1)S(1)}, s32[]{:S(2)}) async-start(s8[9437184]{0:T(1024)(128)(4,1)} %bitcast.180), calls=%async_computation.10 | async-start | bytes 8388608
  205.1 18.5 %slice-start.12 = ((s8[4718592]{0:T(1024)(128)(4,1)}), s8[4194304]{0:T(1024)(128)(4,1)S(1)}, s32[]{:S(2)}) async-start(s8[4718592]{0:T(1024)(128)(4,1)} %bitcast.184), calls=%async_computation.15 | async-start | bytes 8388608
  214.2 9.4 %slice-start.8 = ((s8[9437184]{0:T(1024)(128)(4,1)}), s8[1048576]{0:T(1024)(128)(4,1)S(1)}, s32[]{:S(2)}) async-start(s8[9437184]{0:T(1024)(128)(4,1)} %bitcast.180), calls=%async_computation.11 | async-start | bytes 2097152
  214.3 9.4 %slice-start.13 = ((s8[4718592]{0:T(1024)(128)(4,1)}), s8[524288]{0:T(1024)(128)(4,1)S(1)}, s32[]{:S(2)}) async-start(s8[4718592]{0:T(1024)(128)(4,1)} %bitcast.184), calls=%async_computation.16 | async-start | bytes 1048576
  223.7 12.6 %slice-start.3 = ((s8[9437184]{0:T(1024)(128)(4,1)}), s8[4194304]{0:T(1024)(128)(4,1)S(1)}, s32[]{:S(2)}) async-start(s8[9437184]{0:T(1024)(128)(4,1)} %bitcast.178), calls=%async_computation.6 | async-start | bytes 8388608
  223.7 12.6 %slice-start.4 = ((s8[9437184]{0:T(1024)(128)(4,1)}), s8[4194304]{0:T(1024)(128)(4,1)S(1)}, s32[]{:S(2)}) async-start(s8[9437184]{0:T(1024)(128)(4,1)} %bitcast.178), calls=%async_computation.7 | async-start | bytes 8388608
  223.7 12.6 %slice-start.14 = ((s8[4718592]{0:T(1024)(128)(4,1)}), s8[524288]{0:T(1024)(128)(4,1)S(1)}, s32[]{:S(2)}) async-start(s8[4718592]{0:T(1024)(128)(4,1)} %bitcast.186), calls=%async_computation.17 | async-start | bytes 1048576
  228.8 7.6 %slice-start.5 = ((s8[9437184]{0:T(1024)(128)(4,1)}), s8[1048576]{0:T(1024)(128)(4,1)S(1)}, s32[]{:S(2)}) async-start(s8[9437184]{0:T(1024)(128)(4,1)} %bitcast.178), calls=%async_computation.8 | async-start | bytes 2097152
  228.8 7.6 %slice-start.15 = ((s8[4718592]{0:T(1024)(128)(4,1)}), s8[4194304]{0:T(1024)(128)(4,1)S(1)}, s32[]{:S(2)}) async-start(s8[4718592]{0:T(1024)(128)(4,1)} %bitcast.186), calls=%async_computation.18 | async-start | bytes 8388608
  228.8 12.7 %slice-start = ((s8[9437184]{0:T(1024)(128)(4,1)}), s8[4194304]{0:T(1024)(128)(4,1)S(1)}, s32[]{:S(2)}) async-start(s8[9437184]{0:T(1024)(128)(4,1)} %bitcast.176), calls=%async_computation.3 | async-start | bytes 8388608
  228.8 12.7 %slice-start.1 = ((s8[9437184]{0:T(1024)(128)(4,1)}), s8[4194304]{0:T(1024)(128)(4,1)S(1)}, s32[]{:S(2)}) async-start(s8[9437184]{0:T(1024)(128)(4,1)} %bitcast.176), calls=%async_computation.4 | async-start | bytes 8388608
  236.4 5.1 %slice-start.2 = ((s8[9437184]{0:T(1024)(128)(4,1)}), s8[1048576]{0:T(1024)(128)(4,1)S(1)}, s32[]{:S(2)}) async-start(s8[9437184]{0:T(1024)(128)(4,1)} %bitcast.176), calls=%async_computation.5 | async-start | bytes 2097152
  310.8 11.7 %slice-start.9 = ((s8[9437184]{0:T(1024)(128)(4,1)}), s8[4194304]{0:T(1024)(128)(4,1)S(1)}, s32[]{:S(2)}) async-start(s8[9437184]{0:T(1024)(128)(4,1)} %bitcast.182), calls=%async_computation.12 | async-start | bytes 8388608
  310.8 11.7 %slice-start.16 = ((s8[4718592]{0:T(1024)(128)(4,1)}), s8[4194304]{0:T(1024)(128)(4,1)S(1)}, s32[]{:S(2)}) async-start(s8[4718592]{0:T(1024)(128)(4,1)} %bitcast.188), calls=%async_computation.19 | async-start | bytes 8388608
  312.3 10.2 %slice-start.10 = ((s8[9437184]{0:T(1024)(128)(4,1)}), s8[4194304]{0:T(1024)(128)(4,1)S(1)}, s32[]{:S(2)}) async-start(s8[9437184]{0:T(1024)(128)(4,1)} %bitcast.182), calls=%async_computation.13 | async-start | bytes 8388608
  312.3 10.2 %slice-start.11 = ((s8[9437184]{0:T(1024)(128)(4,1)}), s8[1048576]{0:T(1024)(128)(4,1)S(1)}, s32[]{:S(2)}) async-start(s8[9437184]{0:T(1024)(128)(4,1)} %bitcast.182), calls=%async_computation.14 | async-start | bytes 2097152
  312.3 10.2 %slice-start.17 = ((s8[4718592]{0:T(1024)(128)(4,1)}), s8[524288]{0:T(1024)(128)(4,1)S(1)}, s32[]{:S(2)}) async-start(s8[4718592]{0:T(1024)(128)(4,1)} %bitcast.188), calls=%async_computation.20 | async-start | bytes 1048576
  (2 other events, 1.6 us)
Sparse Core Ops, SparseCore 0:
  10.2 82.0 all-gather.8
  105.3 85.9 all-gather.4
  204.2 85.6 all-gather.6
where the time goes:
time: 336 us
  waiting for transfers between devices  217 us (65%)
  matrix products  93.4 us (28%)
  between operations  14.2 us (4%)
  local copies, waits for them, and re-layouts  5.3 us (2%)
  other arithmetic  3.5 us (1%)
    all_gather x3, waiting for transfers between devices, shards(): piece = lax.all_gather(incoming, 'row', axis=0, tiled=True)  213 us
    dot_general x12, matrix products, shards(): results.append(jnp.dot(matrix, piece, preferred_element_type=jnp.float32))  93.4 us
  transfers between devices with their start and end apart: 5, of which 5 were waited for; matrix products, arithmetic and copies ran while one was open for 13% of the time, Pallas kernels for 0%

commit v1 on v0

v1 whole, which is shorter than its diff:
```python
import functools

import jax
import jax.numpy as jnp
import numpy as np
from jax import lax
from jax.experimental import pallas as pl
from jax.experimental.pallas import tpu as pltpu
from jax.sharding import PartitionSpec as P

ANY = pl.BlockSpec(memory_space=pl.ANY)
SMEM = pl.BlockSpec(memory_space=pltpu.SMEM)


def ring_order(n):
    return list(range(0, n, 2)) + list(range(n - 1, 0, -2))


def owner_table(n):
    order = ring_order(n)
    table = np.zeros((n, n), np.int32)
    for place, r in enumerate(order):
        offsets = [0]
        for s in range(1, n // 2 + 1):
            offsets += [-s, s] if 2 * s < n else [-s]
        for j, o in enumerate(offsets):
            table[r, j] = order[(place + o) % n]
    return table


def ring_hop(x, n, by):
    order = ring_order(n)
    return lax.ppermute(x, "row", [(order[i], order[(i + by) % n]) for i in range(n)])


def accumulate_kernel(places, offsets, carried, finish, tick, own, *refs):
    mats, parts = len(finish), len(places)
    refs = list(refs)
    take = lambda count: [refs.pop(0) for _ in range(count)]
    weights, shards = take(mats), take(parts)
    carry_in = take(mats) if carried else []
    src = take(1)[0] if "send" in finish else None
    sizes = [s.shape[0] for s in shards]
    starts = [sum(sizes[:i]) for i in range(parts)]
    n_out = sum(2 if f == "send" else 1 for f in finish)
    while len(refs) > n_out + 9:
        refs.pop(0)
    outs = take(n_out)
    wbuf, xbuf, acc, stage, xsem, wsem, asem, osem, ssem = refs
    depth = weights[0].shape[1] // (own.shape[1] - 1)
    x_in = [pltpu.make_async_copy(shards[i], xbuf.at[pl.ds(starts[i], sizes[i])], xsem.at[i])
            for i in range(parts)]
    for c in x_in:
        c.start()
    w_in, a_in = [], []
    for m in range(mats):
        row = []
        for i in range(parts):
            first = own[0, places[i]] * depth + offsets[i]
            columns = pl.ds(pl.multiple_of(first, 128), sizes[i])
            row.append(pltpu.make_async_copy(
                weights[m].at[:, columns], wbuf.at[m, :, pl.ds(starts[i], sizes[i])],
                wsem.at[m * parts + i]))
            row[-1].start()
        w_in.append(row)
        if carried:
            a_in.append(pltpu.make_async_copy(carry_in[m], acc.at[m], asem.at[m]))
            a_in[-1].start()
        if finish[m] == "send":
            src_in = pltpu.make_async_copy(src.at[0, tick], stage.at[mats], ssem)
            src_in.start()
    for c in x_in:
        c.wait()
    pending, sem = [], 0
    for m in range(mats):
        for c in w_in[m]:
            c.wait()
        product = jnp.dot(wbuf[m], xbuf[...], preferred_element_type=jnp.float32)
        if carried:
            a_in[m].wait()
            acc[m] = acc[m] + product
        else:
            acc[m] = product
        if finish[m] == "carry":
            copies = [(acc.at[m], outs.pop(0))]
        elif finish[m] == "emit":
            stage[m] = acc[m].astype(stage.dtype)
            copies = [(stage.at[m], outs.pop(0).at[0, tick])]
        else:
            src_in.wait()
            sent = acc[m] + stage[mats].astype(jnp.float32)
            stage[m] = sent.astype(stage.dtype)
            stage[mats] = (sent * own[0, own.shape[1] - 1].astype(jnp.float32)).astype(stage.dtype)
            copies = [(stage.at[mats], outs.pop(0)), (stage.at[m], outs.pop(0))]
        for a, b in copies:
            pending.append(pltpu.make_async_copy(a, b, osem.at[sem]))
            pending[-1].start()
            sem += 1
    for c in pending:
        c.wait()


def accumulate(own, weights, parts, carry, finish, tick, sources, held):
    mats, (rows, unknowns) = len(weights), weights[0].shape
    cols = parts[0][0].shape[1]
    depth = sum(p[0].shape[0] for p in parts)
    args = [own, *weights, *[p[0] for p in parts], *(carry or [])]
    if "send" in finish:
        args.append(sources)
    shapes, aliases = [], {}
    for m, f in enumerate(finish):
        if f == "carry":
            shapes.append(jax.ShapeDtypeStruct((rows, cols), jnp.float32))
        elif f == "emit":
            if held[m] is not None:
                aliases[len(args)] = len(shapes)
                args.append(held[m])
            shapes.append(jax.ShapeDtypeStruct((1, sources.shape[1], rows, cols), jnp.bfloat16))
        else:
            shapes += [jax.ShapeDtypeStruct((rows, cols), jnp.bfloat16)] * 2
    return pl.pallas_call(
        functools.partial(
            accumulate_kernel, tuple(p[1] for p in parts), tuple(p[2] for p in parts),
            bool(carry), tuple(finish), tick),
        out_shape=tuple(shapes),
        in_specs=[SMEM] + [ANY] * (len(args) - 1),
        out_specs=tuple(ANY for _ in shapes),
        input_output_aliases=aliases,
        scratch_shapes=[
            pltpu.VMEM((mats, rows, depth), jnp.bfloat16),
            pltpu.VMEM((depth, cols), jnp.bfloat16),
            pltpu.VMEM((mats, rows, cols), jnp.float32),
            pltpu.VMEM((mats + 1, rows, cols), jnp.bfloat16),
            pltpu.SemaphoreType.DMA((len(parts),)),
            pltpu.SemaphoreType.DMA((len(parts) * mats,)),
            pltpu.SemaphoreType.DMA((mats,)),
            pltpu.SemaphoreType.DMA((mats + 1,)),
            pltpu.SemaphoreType.DMA,
        ],
        compiler_params=pltpu.CompilerParams(vmem_limit_bytes=62 << 20),
        cost_estimate=pl.CostEstimate(
            flops=2 * mats * rows * depth * 512, bytes_accessed=2 * mats * rows * depth,
            transcendentals=0),
    )(*args)


def sweep(layers, n, transmission, reflection, receiver_map, midplane_map, traces, sources):
    ticks = sources.shape[1]
    weights = [transmission[0], reflection[0], receiver_map[0], midplane_map[0]]
    row = lax.dynamic_slice_in_dim(jnp.asarray(owner_table(n)), lax.axis_index("row"), 1, 0)
    passes_on = jnp.where(lax.axis_index("layer") < layers - 1, 1, 0).astype(jnp.int32)
    own = jnp.concatenate([row, passes_on.reshape(1, 1)], axis=1)
    outs = [None] * 3
    incoming = traces[0]
    half = incoming.shape[0] // 2
    around = [(i, (i + 1) % layers) for i in range(layers)]
    last_step = n // 2
    left_over = None

    for tick in range(ticks):
        final = tick + 1 == ticks
        up = down = incoming
        ready = [(incoming, 0, 0)]
        carry = None
        for s in range(1, last_step + 1):
            if s < last_step:
                new_up = ring_hop(up, n, 1)
                new_down = ring_hop(down, n, -1)
                arrived = [(new_up, 2 * s - 1, 0), (new_down, 2 * s, 0)]
            else:
                new_up = ring_hop(up[:half], n, 1)
                new_down = ring_hop(down[half:], n, -1)
                arrived = [(new_up, n - 1, 0), (new_down, n - 1, half)]
            if s == 1:
                if left_over is not None:
                    outs = list(accumulate(own, weights[1:], *left_over, ["emit"] * 3, tick - 1, sources,
                                    outs))
            elif s < last_step or final:
                carry = list(accumulate(own, weights, ready, carry, ["carry"] * 4, tick, sources, None))
                ready = []
            else:
                sums = accumulate(own, weights[:1], ready, carry[:1], ["carry"], tick, sources, None)
                carry = list(sums) + carry[1:]
            ready = ready + arrived
            up, down = new_up, new_down
        if final:
            res = accumulate(own, weights, ready, carry, ["send"] + ["emit"] * 3, tick, sources,
                      [None] + outs)
            return res[2], res[3], res[4], res[1][None]
        passed, _ = accumulate(own, weights[:1], arrived, carry[:1], ["send"], tick, sources, None)
        left_over = (ready, carry[1:])
        incoming = lax.ppermute(passed, "layer", around)


def plain_program(layers, transmission, reflection, receiver_map, midplane_map, traces, sources):
    incoming = sent = traces[0]
    outs = [[], [], []]
    for tick in range(sources.shape[1]):
        piece = lax.all_gather(incoming, "row", axis=0, tiled=True)
        total = jnp.dot(transmission[0], piece, preferred_element_type=jnp.float32)
        sent = (total + sources[0, tick].astype(jnp.float32)).astype(jnp.bfloat16)
        for out, w in zip(outs, (reflection, receiver_map, midplane_map)):
            out.append(jnp.dot(w[0], piece, preferred_element_type=jnp.float32).astype(jnp.bfloat16))
        incoming = lax.ppermute(sent, "layer", [(i, i + 1) for i in range(layers - 1)])
    return tuple(jnp.stack(o)[None] for o in outs) + (sent[None],)


def solution(mesh):
    layers, n = mesh.shape["layer"], mesh.shape["row"]

    def body(transmission, reflection, receiver_map, midplane_map, traces, sources):
        args = (transmission, reflection, receiver_map, midplane_map, traces, sources)
        if traces.shape[1] % 256 or n % 2 or n < 4:
            return plain_program(layers, *args)
        return sweep(layers, n, *args)

    wide = P("layer", "row", None)
    deep = P("layer", None, "row", None)
    return jax.shard_map(
        body,
        mesh=mesh,
        in_specs=(wide, wide, wide, wide, wide, deep),
        out_specs=(deep, deep, deep, wide),
        check_vma=False,
    )
```

time: 336 us -> 272 us (0.81); the launches traced: 336 us -> 267 us
  Pallas kernels: 0 us -> 150 us
  waiting for transfers between devices: 217 us -> 79.1 us
  matrix products: 93.4 us -> 0 us
  starting transfers between devices: 2.77 us -> 27 us
  between operations: 14.2 us -> 1.25 us
  local copies, waits for them, and re-layouts: 5.3 us -> 8.98 us
    all_gather x3 -> x0, waiting for transfers between devices: 213 us -> none  [shards(): piece = lax.all_gather(incoming, 'row', axis=0, tiled=True)]
    pallas_call x0 -> x14, Pallas kernels: none -> 150 us  [accumulate(): pl.pallas_call(functools.partial(accumulate_kernel, tuple((p[1] for p in...]
    dot_general x12 -> x0, matrix products: 93.4 us -> none  [shards(): results.append(jnp.dot(matrix, piece, preferred_element_type=jnp.float32))]
    ppermute x2 -> x26, waiting for transfers between devices: 3.15 us -> 79.1 us  [the longest x24 60.1 us: ring_hop(): lax.ppermute(x, 'row', [(order[i], order[(i + by) % n]) for i in range(n)])]
    ppermute x2 -> x26, starting transfers between devices: 2.65 us -> 27 us  [the longest x24 26.9 us: ring_hop(): lax.ppermute(x, 'row', [(order[i], order[(i + by) % n]) for i in range(n)])]
    slice x1 -> x6, local copies, waits for them, and re-layouts: 0.12 us -> 4.19 us  [the longest x3 2.53 us: sweep(): new_up = ring_hop(up[:half], n, 1)]
    broadcast_in_dim x2 -> x0, other arithmetic: 3.5 us -> none  [the longest x1 2.06 us: shards(): jnp.stack(bounced_all, axis=0)[None]]
  transfers between devices with their start and end apart: 5 -> 26, of which waited for: 5 -> 8; matrix products, arithmetic and copies ran while one was open for 13% -> 2% of each run, Pallas kernels for 0% -> 50%
where the time goes in v1:
time: 272 us; the launch traced here: 267 us
  Pallas kernels  150 us (55%)
  waiting for transfers between devices  79.1 us (29%)
  starting transfers between devices  27 us (10%)
  local copies, waits for them, and re-layouts  8.98 us (3%)
    pallas_call x14, Pallas kernels, accumulate(): pl.pallas_call(functools.partial(accumulate_kernel, tuple((p[1] for p in...  150 us
    ppermute x24, waiting for transfers between devices, ring_hop(): lax.ppermute(x, 'row', [(order[i], order[(i + by) % n]) for i in range(n)])  60.1 us
    ppermute x24, starting transfers between devices, ring_hop(): lax.ppermute(x, 'row', [(order[i], order[(i + by) % n]) for i in range(n)])  26.9 us
    ppermute x2, waiting for transfers between devices, sweep(): incoming = lax.ppermute(passed, 'layer', around)  19 us
  transfers between devices with their start and end apart: 26, of which 8 were waited for; matrix products, arithmetic and copies ran while one was open for 2% of the time, Pallas kernels for 50%

profile of v1, /device:TPU:0, one launch (start us, length us, event | category | flops | bytes accessed | tf_op | source)
XLA Modules:
  0.0 267.4 jit_solution(2945487056666822404)
XLA Ops:
  0.6 3.1 %collective-permute-start = (bf16[768,384]{1,0:T(8,128)(2,1)}, bf16[768,384]{1,0:T(8,128)(2,1)S(1)}, u32[]{:S(2)}, u32[]{:S(2)}) collective-permute-start(bf16[768,384]{1,0:T(8,128)(2,1)} %bitcast.49), channel_id=1, source_target_pairs={{0,2},{2,4},{4,6},{6,7},{7,5},{5,3},{3,1},{1,0},{8,10},{10,12},{12... | collective-permute-start | bytes 1769480 | tf_op jit(solution)/shard_map/ppermute | solution.py:33
  3.7 13.5 %collective-permute-done.refs_5_ = bf16[768,384]{1,0:T(8,128)(2,1)S(1)} collective-permute-done((bf16[768,384]{1,0:T(8,128)(2,1)}, bf16[768,384]{1,0:T(8,128)(2,1)S(1)}, u32[]{:S(2)}, u32[]{:S(2)}) %collective-permute-start) | collective-permute-done | bytes 589856 | tf_op jit(solution)/shard_map/ppermute | solution.py:33
  20.6 11.1 %collective-permute-done.1.refs_4_ = bf16[768,384]{1,0:T(8,128)(2,1)S(1)} collective-permute-done((bf16[768,384]{1,0:T(8,128)(2,1)S(1)}, bf16[768,384]{1,0:T(8,128)(2,1)S(1)}, u32[]{:S(2)}, u32[]{:S(2)}) %collective-permute-start.1) | collective-permute-done | bytes 589856 | tf_op jit(solution)/shard_map/ppermute | solution.py:33
  33.8 15.1 %shard_map.102 = (f32[768,384]{1,0:T(8,128)}, f32[768,384]{1,0:T(8,128)}, f32[768,384]{1,0:T(8,128)}, f32[768,384]{1,0:T(8,128)}) custom-call(s32[1,9]{1,0:T(1,128)} %pad_add_fusion.own, bf16[768,6144]{1,0:T(8,128)(2,1)} %bitcast.7, bf16[768,6144]{1,0:T(8,128)(2,1)} %bitcast.19, bf16[768,6144]{1,0:T(8,128)(2,1)} %bitcast.29, bf16[768,6144]{1,0:T(8,128)(2,1)} %bitcast.39, ...), custom_call_target="tpu_custom_call" | custom-call | flops 7247757312 | bytes 14155776 | tf_op jit(solution)/shard_map/pallas_call | solution.py:121
  52.8 12.6 %shard_map.103 = (f32[768,384]{1,0:T(8,128)}, f32[768,384]{1,0:T(8,128)}, f32[768,384]{1,0:T(8,128)}, f32[768,384]{1,0:T(8,128)}) custom-call(s32[1,9]{1,0:T(1,128)} %pad_add_fusion.own, bf16[768,6144]{1,0:T(8,128)(2,1)} %bitcast.8, bf16[768,6144]{1,0:T(8,128)(2,1)} %bitcast.20, bf16[768,6144]{1,0:T(8,128)(2,1)} %bitcast.30, bf16[768,6144]{1,0:T(8,128)(2,1)} %bitcast.40, ...), custom_call_target="tpu_custom_call" | custom-call | flops 4831838208 | bytes 9437184 | tf_op jit(solution)/shard_map/pallas_call | solution.py:121
  65.4 5.2 %shard_map.104.refs_3_ = f32[768,384]{1,0:T(8,128)} custom-call(s32[1,9]{1,0:T(1,128)} %pad_add_fusion.own, bf16[768,6144]{1,0:T(8,128)(2,1)} %bitcast.9, bf16[768,384]{1,0:T(8,128)(2,1)} %copy-done, bf16[768,384]{1,0:T(8,128)(2,1)} %copy-done.1, f32[768,384]{1,0:T(8,128)} %get-tuple-element.48.refs_3_), custom_call_target="tpu_custom_call" | custom-call | flops 1207959552 | bytes 2359296 | tf_op jit(solution)/shard_map/pallas_call | solution.py:121
  72.1 4.2 %shard_map.105 = (bf16[768,384]{1,0:T(8,128)(2,1)}, bf16[768,384]{1,0:T(8,128)(2,1)}) custom-call(s32[1,9]{1,0:T(1,128)} %pad_add_fusion.own, bf16[768,6144]{1,0:T(8,128)(2,1)} %bitcast.10, bf16[384,384]{1,0:T(8,128)(2,1)} %copy-done.6, bf16[384,384]{1,0:T(8,128)(2,1)} %copy-done.7, f32[768,384]{1,0:T(8,128)} %shard_map.104.refs_3_, ...), custom_call_target="tpu_custom_call" | custom-call | flops 603979776 | bytes 1179648 | tf_op jit(solution)/shard_map/pallas_call | solution.py:121
  76.4 9.5 %collective-permute-done.8.refs_4_ = bf16[768,384]{1,0:T(8,128)(2,1)S(1)} collective-permute-done((bf16[768,384]{1,0:T(8,128)(2,1)}, bf16[768,384]{1,0:T(8,128)(2,1)S(1)}, u32[]{:S(2)}, u32[]{:S(2)}) %collective-permute-start.8) | collective-permute-done | bytes 589856 | tf_op jit(solution)/shard_map/ppermute | solution.py:192
  87.9 12.4 %collective-permute-done.9.refs_5_ = bf16[768,384]{1,0:T(8,128)(2,1)S(1)} collective-permute-done((bf16[768,384]{1,0:T(8,128)(2,1)S(1)}, bf16[768,384]{1,0:T(8,128)(2,1)S(1)}, u32[]{:S(2)}, u32[]{:S(2)}) %collective-permute-start.9) | collective-permute-done | bytes 589856 | tf_op jit(solution)/shard_map/ppermute | solution.py:33
  102.4 11.9 %collective-permute-done.10.refs_4_ = bf16[768,384]{1,0:T(8,128)(2,1)S(1)} collective-permute-done((bf16[768,384]{1,0:T(8,128)(2,1)S(1)}, bf16[768,384]{1,0:T(8,128)(2,1)S(1)}, u32[]{:S(2)}, u32[]{:S(2)}) %collective-permute-start.10) | collective-permute-done | bytes 589856 | tf_op jit(solution)/shard_map/ppermute | solution.py:33
  116.6 15.1 %shard_map.106 = (f32[768,384]{1,0:T(8,128)}, f32[768,384]{1,0:T(8,128)}, f32[768,384]{1,0:T(8,128)}, f32[768,384]{1,0:T(8,128)}) custom-call(s32[1,9]{1,0:T(1,128)} %pad_add_fusion.own, bf16[768,6144]{1,0:T(8,128)(2,1)} %bitcast.11, bf16[768,6144]{1,0:T(8,128)(2,1)} %bitcast.21, bf16[768,6144]{1,0:T(8,128)(2,1)} %bitcast.31, bf16[768,6144]{1,0:T(8,128)(2,1)} %bitcast.41, ...), custom_call_target="tpu_custom_call" | custom-call | flops 7247757312 | bytes 14155776 | tf_op jit(solution)/shard_map/pallas_call | solution.py:121
  135.5 12.6 %shard_map.107 = (f32[768,384]{1,0:T(8,128)}, f32[768,384]{1,0:T(8,128)}, f32[768,384]{1,0:T(8,128)}, f32[768,384]{1,0:T(8,128)}) custom-call(s32[1,9]{1,0:T(1,128)} %pad_add_fusion.own, bf16[768,6144]{1,0:T(8,128)(2,1)} %bitcast.12, bf16[768,6144]{1,0:T(8,128)(2,1)} %bitcast.22, bf16[768,6144]{1,0:T(8,128)(2,1)} %bitcast.32, bf16[768,6144]{1,0:T(8,128)(2,1)} %bitcast.42, ...), custom_call_target="tpu_custom_call" | custom-call | flops 4831838208 | bytes 9437184 | tf_op jit(solution)/shard_map/pallas_call | solution.py:121
  148.2 5.2 %shard_map.108.refs_3_ = f32[768,384]{1,0:T(8,128)} custom-call(s32[1,9]{1,0:T(1,128)} %pad_add_fusion.own, bf16[768,6144]{1,0:T(8,128)(2,1)} %bitcast.13, bf16[768,384]{1,0:T(8,128)(2,1)} %copy-done.2, bf16[768,384]{1,0:T(8,128)(2,1)} %copy-done.3, f32[768,384]{1,0:T(8,128)} %get-tuple-element.54.refs_3_), custom_call_target="tpu_custom_call" | custom-call | flops 1207959552 | bytes 2359296 | tf_op jit(solution)/shard_map/pallas_call | solution.py:121
  154.9 4.2 %shard_map.109 = (bf16[768,384]{1,0:T(8,128)(2,1)}, bf16[768,384]{1,0:T(8,128)(2,1)}) custom-call(s32[1,9]{1,0:T(1,128)} %pad_add_fusion.own, bf16[768,6144]{1,0:T(8,128)(2,1)} %bitcast.14, bf16[384,384]{1,0:T(8,128)(2,1)} %copy-done.8, bf16[384,384]{1,0:T(8,128)(2,1)} %copy-done.9, f32[768,384]{1,0:T(8,128)} %shard_map.108.refs_3_, ...), custom_call_target="tpu_custom_call" | custom-call | flops 603979776 | bytes 1179648 | tf_op jit(solution)/shard_map/pallas_call | solution.py:121
  159.2 9.5 %collective-permute-done.17.refs_4_ = bf16[768,384]{1,0:T(8,128)(2,1)S(1)} collective-permute-done((bf16[768,384]{1,0:T(8,128)(2,1)}, bf16[768,384]{1,0:T(8,128)(2,1)S(1)}, u32[]{:S(2)}, u32[]{:S(2)}) %collective-permute-start.17) | collective-permute-done | bytes 589856 | tf_op jit(solution)/shard_map/ppermute | solution.py:192
  171.2 10.7 %collective-permute-done.18.refs_5_ = bf16[768,384]{1,0:T(8,128)(2,1)S(1)} collective-permute-done((bf16[768,384]{1,0:T(8,128)(2,1)S(1)}, bf16[768,384]{1,0:T(8,128)(2,1)S(1)}, u32[]{:S(2)}, u32[]{:S(2)}) %collective-permute-start.18) | collective-permute-done | bytes 589856 | tf_op jit(solution)/shard_map/ppermute | solution.py:33
  184.2 13.3 %shard_map.113 = (bf16[1,3,768,384]{3,2,1,0:T(8,128)(2,1)}, bf16[1,3,768,384]{3,2,1,0:T(8,128)(2,1)}, bf16[1,3,768,384]{3,2,1,0:T(8,128)(2,1)}) custom-call(s32[1,9]{1,0:T(1,128)} %pad_add_fusion.own, bf16[768,6144]{1,0:T(8,128)(2,1)} %bitcast.23, bf16[768,6144]{1,0:T(8,128)(2,1)} %bitcast.33, bf16[768,6144]{1,0:T(8,128)(2,1)} %bitcast.43, ...), custom_call_target="tpu_custom_call" | custom-call | flops 5435817984 | bytes 10616832 | tf_op jit(solution)/shard_map/pallas_call | solution.py:121
  197.5 13.3 %shard_map.114 = (bf16[1,3,768,384]{3,2,1,0:T(8,128)(2,1)}, bf16[1,3,768,384]{3,2,1,0:T(8,128)(2,1)}, bf16[1,3,768,384]{3,2,1,0:T(8,128)(2,1)}) custom-call(s32[1,9]{1,0:T(1,128)} %pad_add_fusion.own, bf16[768,6144]{1,0:T(8,128)(2,1)} %bitcast.24, bf16[768,6144]{1,0:T(8,128)(2,1)} %bitcast.34, ...), custom_call_target="tpu_custom_call", output_to_operand_aliasing={{0}: (11, {}), {1}: (12, {}), {2}: (13, {})} | custom-call | flops 5435817984 | bytes 10616832 | tf_op jit(solution)/shard_map/pallas_call | solution.py:121
  210.8 2.2 collective-permute-start.20
  213.4 15.2 %shard_map.110 = (f32[768,384]{1,0:T(8,128)}, f32[768,384]{1,0:T(8,128)}, f32[768,384]{1,0:T(8,128)}, f32[768,384]{1,0:T(8,128)}) custom-call(s32[1,9]{1,0:T(1,128)} %pad_add_fusion.own, bf16[768,6144]{1,0:T(8,128)(2,1)} %bitcast.15, bf16[768,6144]{1,0:T(8,128)(2,1)} %bitcast.25, bf16[768,6144]{1,0:T(8,128)(2,1)} %bitcast.35, bf16[768,6144]{1,0:T(8,128)(2,1)} %bitcast.45, ...), custom_call_target="tpu_custom_call" | custom-call | flops 7247757312 | bytes 14155776 | tf_op jit(solution)/shard_map/pallas_call | solution.py:121
  228.6 12.7 %shard_map.111 = (f32[768,384]{1,0:T(8,128)}, f32[768,384]{1,0:T(8,128)}, f32[768,384]{1,0:T(8,128)}, f32[768,384]{1,0:T(8,128)}) custom-call(s32[1,9]{1,0:T(1,128)} %pad_add_fusion.own, bf16[768,6144]{1,0:T(8,128)(2,1)} %bitcast.16, bf16[768,6144]{1,0:T(8,128)(2,1)} %bitcast.26, bf16[768,6144]{1,0:T(8,128)(2,1)} %bitcast.36, bf16[768,6144]{1,0:T(8,128)(2,1)} %bitcast.46, ...), custom_call_target="tpu_custom_call" | custom-call | flops 4831838208 | bytes 9437184 | tf_op jit(solution)/shard_map/pallas_call | solution.py:121
  242.1 1.9 collective-permute-start.21
  244.9 12.6 %shard_map.112 = (f32[768,384]{1,0:T(8,128)}, f32[768,384]{1,0:T(8,128)}, f32[768,384]{1,0:T(8,128)}, f32[768,384]{1,0:T(8,128)}) custom-call(s32[1,9]{1,0:T(1,128)} %pad_add_fusion.own, bf16[768,6144]{1,0:T(8,128)(2,1)} %bitcast.17, bf16[768,6144]{1,0:T(8,128)(2,1)} %bitcast.27, bf16[768,6144]{1,0:T(8,128)(2,1)} %bitcast.37, bf16[768,6144]{1,0:T(8,128)(2,1)} %bitcast.47, ...), custom_call_target="tpu_custom_call" | custom-call | flops 4831838208 | bytes 9437184 | tf_op jit(solution)/shard_map/pallas_call | solution.py:121
  258.2 8.9 %shard_map.115 = (bf16[768,384]{1,0:T(8,128)(2,1)}, bf16[768,384]{1,0:T(8,128)(2,1)}, bf16[1,3,768,384]{3,2,1,0:T(8,128)(2,1)}, bf16[1,3,768,384]{3,2,1,0:T(8,128)(2,1)}, bf16[1,3,768,384]{3,2,1,0:T(8,128)(2,1)}) custom-call(s32[1,9]{1,0:T(1,128)} %pad_add_fusion.own, ...), custom_call_target="tpu_custom_call", output_to_operand_aliasing={{2}: (12, {}), {3}: (13, {}), {4}: (14, {})} | custom-call | flops 2415919104 | bytes 4718592 | tf_op jit(solution)/shard_map/pallas_call | solution.py:121
  (94 shorter events, 29.9 us)
Async XLA Ops:
  0.6 16.6 %collective-permute-start = (bf16[768,384]{1,0:T(8,128)(2,1)}, bf16[768,384]{1,0:T(8,128)(2,1)S(1)}, u32[]{:S(2)}, u32[]{:S(2)}) collective-permute-start(bf16[768,384]{1,0:T(8,128)(2,1)} %bitcast.49), channel_id=1, source_target_pairs={{0,2},{2,4},{4,6},{6,7},{7,5},{5,3},{3,1},{1,0},{8,10},{10,12},{12... | collective-permute-start | bytes 1769480 | tf_op jit(solution)/shard_map/ppermute | solution.py:33
  3.7 15.3 %collective-permute-start.4 = (bf16[768,384]{1,0:T(8,128)(2,1)}, bf16[768,384]{1,0:T(8,128)(2,1)S(1)}, u32[]{:S(2)}, u32[]{:S(2)}) collective-permute-start(bf16[768,384]{1,0:T(8,128)(2,1)} %bitcast.50), channel_id=1, source_target_pairs={{0,1},{2,0},{4,2},{6,4},{7,6},{5,7},{3,5},{1,3},{8,9},{10,8},{12,1... | collective-permute-start | bytes 1769480 | tf_op jit(solution)/shard_map/ppermute | solution.py:33
  17.2 14.5 %collective-permute-start.1 = (bf16[768,384]{1,0:T(8,128)(2,1)S(1)}, bf16[768,384]{1,0:T(8,128)(2,1)S(1)}, u32[]{:S(2)}, u32[]{:S(2)}) collective-permute-start(bf16[768,384]{1,0:T(8,128)(2,1)S(1)} %collective-permute-done.refs_5_), channel_id=1, source_target_pairs={{0,2},{2,4},{4,6},{6,7},{7,5},{5,3},{3,1},{1,0},{8,10},{10,12},{12... | collective-permute-start | bytes 1769480 | tf_op jit(solution)/shard_map/ppermute | solution.py:33
  19.0 14.2 %collective-permute-start.5 = (bf16[768,384]{1,0:T(8,128)(2,1)S(1)}, bf16[768,384]{1,0:T(8,128)(2,1)}, u32[]{:S(2)}, u32[]{:S(2)}) collective-permute-start(bf16[768,384]{1,0:T(8,128)(2,1)S(1)} %collective-permute-done.4.refs_6_), channel_id=1, source_target_pairs={{0,1},{2,0},{4,2},{6,4},{7,6},{5,7},{3,5},{1,3},{8,9},{10,8},{12,1... | collective-permute-start | bytes 1769480 | tf_op jit(solution)/shard_map/ppermute | solution.py:33
  31.7 17.3 %collective-permute-start.2 = (bf16[768,384]{1,0:T(8,128)(2,1)S(1)}, bf16[768,384]{1,0:T(8,128)(2,1)S(1)}, u32[]{:S(2)}, u32[]{:S(2)}) collective-permute-start(bf16[768,384]{1,0:T(8,128)(2,1)S(1)} %collective-permute-done.1.refs_4_), channel_id=1, source_target_pairs={{0,2},{2,4},{4,6},{6,7},{7,5},{5,3},{3,1},{1,0},{8,10},{10,12},{12... | collective-permute-start | bytes 1769480 | tf_op jit(solution)/shard_map/ppermute | solution.py:33
  33.2 18.1 %collective-permute-start.6 = (bf16[768,384]{1,0:T(8,128)(2,1)}, bf16[768,384]{1,0:T(8,128)(2,1)S(1)}, u32[]{:S(2)}, u32[]{:S(2)}) collective-permute-start(bf16[768,384]{1,0:T(8,128)(2,1)} %collective-permute-done.5.refs_5_), channel_id=1, source_target_pairs={{0,1},{2,0},{4,2},{6,4},{7,6},{5,7},{3,5},{1,3},{8,9},{10,8},{12,1... | collective-permute-start | bytes 1769480 | tf_op jit(solution)/shard_map/ppermute | solution.py:33
  49.8 20.9 %collective-permute-start.3 = (bf16[384,384]{1,0:T(8,128)(2,1)}, bf16[384,384]{1,0:T(8,128)(2,1)S(1)}, u32[]{:S(2)}, u32[]{:S(2)}) collective-permute-start(bf16[384,384]{1,0:T(8,128)(2,1)} %slice.24), channel_id=1, source_target_pairs={{0,2},{2,4},{4,6},{6,7},{7,5},{5,3},{3,1},{1,0},{8,10},{10,12},{12... | collective-permute-start | bytes 884744 | tf_op jit(solution)/shard_map/ppermute | solution.py:33
  52.1 18.5 %collective-permute-start.7 = (bf16[384,384]{1,0:T(8,128)(2,1)}, bf16[384,384]{1,0:T(8,128)(2,1)S(1)}, u32[]{:S(2)}, u32[]{:S(2)}) collective-permute-start(bf16[384,384]{1,0:T(8,128)(2,1)} %slice.25), channel_id=1, source_target_pairs={{0,1},{2,0},{4,2},{6,4},{7,6},{5,7},{3,5},{1,3},{8,9},{10,8},{12,1... | collective-permute-start | bytes 884744 | tf_op jit(solution)/shard_map/ppermute | solution.py:33
  85.9 14.5 %collective-permute-start.9 = (bf16[768,384]{1,0:T(8,128)(2,1)S(1)}, bf16[768,384]{1,0:T(8,128)(2,1)S(1)}, u32[]{:S(2)}, u32[]{:S(2)}) collective-permute-start(bf16[768,384]{1,0:T(8,128)(2,1)S(1)} %collective-permute-done.8.refs_4_), channel_id=1, source_target_pairs={{0,2},{2,4},{4,6},{6,7},{7,5},{5,3},{3,1},{1,0},{8,10},{10,12},{12... | collective-permute-start | bytes 1769480 | tf_op jit(solution)/shard_map/ppermute | solution.py:33
  87.5 14.5 %collective-permute-start.13 = (bf16[768,384]{1,0:T(8,128)(2,1)S(1)}, bf16[768,384]{1,0:T(8,128)(2,1)S(1)}, u32[]{:S(2)}, u32[]{:S(2)}) collective-permute-start(bf16[768,384]{1,0:T(8,128)(2,1)S(1)} %collective-permute-done.8.refs_4_), channel_id=1, source_target_pairs={{0,1},{2,0},{4,2},{6,4},{7,6},{5,7},{3,5},{1,3},{8,9},{10,8},{12,1... | collective-permute-start | bytes 1769480 | tf_op jit(solution)/shard_map/ppermute | solution.py:33
  100.4 13.9 %collective-permute-start.10 = (bf16[768,384]{1,0:T(8,128)(2,1)S(1)}, bf16[768,384]{1,0:T(8,128)(2,1)S(1)}, u32[]{:S(2)}, u32[]{:S(2)}) collective-permute-start(bf16[768,384]{1,0:T(8,128)(2,1)S(1)} %collective-permute-done.9.refs_5_), channel_id=1, source_target_pairs={{0,2},{2,4},{4,6},{6,7},{7,5},{5,3},{3,1},{1,0},{8,10},{10,12},{12... | collective-permute-start | bytes 1769480 | tf_op jit(solution)/shard_map/ppermute | solution.py:33
  102.0 13.6 %collective-permute-start.14 = (bf16[768,384]{1,0:T(8,128)(2,1)S(1)}, bf16[768,384]{1,0:T(8,128)(2,1)}, u32[]{:S(2)}, u32[]{:S(2)}) collective-permute-start(bf16[768,384]{1,0:T(8,128)(2,1)S(1)} %collective-permute-done.13.refs_6_), channel_id=1, source_target_pairs={{0,1},{2,0},{4,2},{6,4},{7,6},{5,7},{3,5},{1,3},{8,9},{10,8},{12,1... | collective-permute-start | bytes 1769480 | tf_op jit(solution)/shard_map/ppermute | solution.py:33
  114.3 17.5 %collective-permute-start.11 = (bf16[768,384]{1,0:T(8,128)(2,1)S(1)}, bf16[768,384]{1,0:T(8,128)(2,1)S(1)}, u32[]{:S(2)}, u32[]{:S(2)}) collective-permute-start(bf16[768,384]{1,0:T(8,128)(2,1)S(1)} %collective-permute-done.10.refs_4_), channel_id=1, source_target_pairs={{0,2},{2,4},{4,6},{6,7},{7,5},{5,3},{3,1},{1,0},{8,10},{10,12},{12... | collective-permute-start | bytes 1769480 | tf_op jit(solution)/shard_map/ppermute | solution.py:33
  115.7 18.3 %collective-permute-start.15 = (bf16[768,384]{1,0:T(8,128)(2,1)}, bf16[768,384]{1,0:T(8,128)(2,1)S(1)}, u32[]{:S(2)}, u32[]{:S(2)}) collective-permute-start(bf16[768,384]{1,0:T(8,128)(2,1)} %collective-permute-done.14.refs_5_), channel_id=1, source_target_pairs={{0,1},{2,0},{4,2},{6,4},{7,6},{5,7},{3,5},{1,3},{8,9},{10,8},{12,1... | collective-permute-start | bytes 1769480 | tf_op jit(solution)/shard_map/ppermute | solution.py:33
  132.7 20.8 %collective-permute-start.12 = (bf16[384,384]{1,0:T(8,128)(2,1)}, bf16[384,384]{1,0:T(8,128)(2,1)S(1)}, u32[]{:S(2)}, u32[]{:S(2)}) collective-permute-start(bf16[384,384]{1,0:T(8,128)(2,1)} %slice.26), channel_id=1, source_target_pairs={{0,2},{2,4},{4,6},{6,7},{7,5},{5,3},{3,1},{1,0},{8,10},{10,12},{12... | collective-permute-start | bytes 884744 | tf_op jit(solution)/shard_map/ppermute | solution.py:33
  134.8 18.6 %collective-permute-start.16 = (bf16[384,384]{1,0:T(8,128)(2,1)}, bf16[384,384]{1,0:T(8,128)(2,1)S(1)}, u32[]{:S(2)}, u32[]{:S(2)}) collective-permute-start(bf16[384,384]{1,0:T(8,128)(2,1)} %slice.27), channel_id=1, source_target_pairs={{0,1},{2,0},{4,2},{6,4},{7,6},{5,7},{3,5},{1,3},{8,9},{10,8},{12,1... | collective-permute-start | bytes 884744 | tf_op jit(solution)/shard_map/ppermute | solution.py:33
  168.8 13.1 %collective-permute-start.18 = (bf16[768,384]{1,0:T(8,128)(2,1)S(1)}, bf16[768,384]{1,0:T(8,128)(2,1)S(1)}, u32[]{:S(2)}, u32[]{:S(2)}) collective-permute-start(bf16[768,384]{1,0:T(8,128)(2,1)S(1)} %collective-permute-done.17.refs_4_), channel_id=1, source_target_pairs={{0,2},{2,4},{4,6},{6,7},{7,5},{5,3},{3,1},{1,0},{8,10},{10,12},{12... | collective-permute-start | bytes 1769480 | tf_op jit(solution)/shard_map/ppermute | solution.py:33
  170.2 13.9 %collective-permute-start.22 = (bf16[768,384]{1,0:T(8,128)(2,1)S(1)}, bf16[768,384]{1,0:T(8,128)(2,1)S(1)}, u32[]{:S(2)}, u32[]{:S(2)}) collective-permute-start(bf16[768,384]{1,0:T(8,128)(2,1)S(1)} %collective-permute-done.17.refs_4_), channel_id=1, source_target_pairs={{0,1},{2,0},{4,2},{6,4},{7,6},{5,7},{3,5},{1,3},{8,9},{10,8},{12,1... | collective-permute-start | bytes 1769480 | tf_op jit(solution)/shard_map/ppermute | solution.py:33
  181.9 28.9 %collective-permute-start.19 = (bf16[768,384]{1,0:T(8,128)(2,1)S(1)}, bf16[768,384]{1,0:T(8,128)(2,1)}, u32[]{:S(2)}, u32[]{:S(2)}) collective-permute-start(bf16[768,384]{1,0:T(8,128)(2,1)S(1)} %collective-permute-done.18.refs_5_), channel_id=1, source_target_pairs={{0,2},{2,4},{4,6},{6,7},{7,5},{5,3},{3,1},{1,0},{8,10},{10,12},{12... | collective-permute-start | bytes 1769480 | tf_op jit(solution)/shard_map/ppermute | solution.py:33
  184.1 28.9 %collective-permute-start.23 = (bf16[768,384]{1,0:T(8,128)(2,1)S(1)}, bf16[768,384]{1,0:T(8,128)(2,1)S(1)}, u32[]{:S(2)}, u32[]{:S(2)}) collective-permute-start(bf16[768,384]{1,0:T(8,128)(2,1)S(1)} %collective-permute-done.22.refs_6_), channel_id=1, source_target_pairs={{0,1},{2,0},{4,2},{6,4},{7,6},{5,7},{3,5},{1,3},{8,9},{10,8},{12,1... | collective-permute-start | bytes 1769480 | tf_op jit(solution)/shard_map/ppermute | solution.py:33
  210.8 30.4 %collective-permute-start.20 = (bf16[768,384]{1,0:T(8,128)(2,1)}, bf16[768,384]{1,0:T(8,128)(2,1)S(1)}, u32[]{:S(2)}, u32[]{:S(2)}) collective-permute-start(bf16[768,384]{1,0:T(8,128)(2,1)} %collective-permute-done.19.refs_4_), channel_id=1, source_target_pairs={{0,2},{2,4},{4,6},{6,7},{7,5},{5,3},{3,1},{1,0},{8,10},{10,12},{12... | collective-permute-start | bytes 1769480 | tf_op jit(solution)/shard_map/ppermute | solution.py:33
  213.1 31.0 %collective-permute-start.24 = (bf16[768,384]{1,0:T(8,128)(2,1)S(1)}, bf16[768,384]{1,0:T(8,128)(2,1)S(1)}, u32[]{:S(2)}, u32[]{:S(2)}) collective-permute-start(bf16[768,384]{1,0:T(8,128)(2,1)S(1)} %collective-permute-done.23.refs_5_), channel_id=1, source_target_pairs={{0,1},{2,0},{4,2},{6,4},{7,6},{5,7},{3,5},{1,3},{8,9},{10,8},{12,1... | collective-permute-start | bytes 1769480 | tf_op jit(solution)/shard_map/ppermute | solution.py:33
  242.1 15.4 %collective-permute-start.21 = (bf16[384,384]{1,0:T(8,128)(2,1)}, bf16[384,384]{1,0:T(8,128)(2,1)}, u32[]{:S(2)}, u32[]{:S(2)}) collective-permute-start(bf16[384,384]{1,0:T(8,128)(2,1)} %slice.28), channel_id=1, source_target_pairs={{0,2},{2,4},{4,6},{6,7},{7,5},{5,3},{3,1},{1,0},{8,10},{10,12},{12... | collective-permute-start | bytes 884744 | tf_op jit(solution)/shard_map/ppermute | solution.py:33
  244.1 13.4 %collective-permute-start.25 = (bf16[384,384]{1,0:T(8,128)(2,1)S(1)}, bf16[384,384]{1,0:T(8,128)(2,1)S(1)}, u32[]{:S(2)}, u32[]{:S(2)}) collective-permute-start(bf16[384,384]{1,0:T(8,128)(2,1)S(1)} %slice.29), channel_id=1, source_target_pairs={{0,1},{2,0},{4,2},{6,4},{7,6},{5,7},{3,5},{1,3},{8,9},{10,8},{12,1... | collective-permute-start | bytes 884744 | tf_op jit(solution)/shard_map/ppermute | solution.py:33
  (24 other events, 270.9 us)

commit v2 on v1

v2 whole, which is shorter than its diff:
```python
import functools

import jax
import jax.numpy as jnp
import numpy as np
from jax import lax
from jax.experimental import pallas as pl
from jax.experimental.pallas import tpu as pltpu
from jax.sharding import PartitionSpec as P

ANY = pl.BlockSpec(memory_space=pl.ANY)
VMEM = pl.BlockSpec(memory_space=pltpu.VMEM)
SMEM = pl.BlockSpec(memory_space=pltpu.SMEM)


def ring_order(n):
    return list(range(0, n, 2)) + list(range(n - 1, 0, -2))


def owner_table(n):
    order = ring_order(n)
    table = np.zeros((n, n), np.int32)
    for place, r in enumerate(order):
        offsets = [0]
        for s in range(1, n // 2 + 1):
            offsets += [-s, s] if 2 * s < n else [-s]
        for j, o in enumerate(offsets):
            table[r, j] = order[(place + o) % n]
    return table


def ring_hop(x, n, by):
    order = ring_order(n)
    return lax.ppermute(x, "row", [(order[i], order[(i + by) % n]) for i in range(n)])


def accumulate_kernel(places, offsets, sums_in, first, finish, tick, blocks, own, *refs):
    mats, parts = len(finish), len(places)
    refs = list(refs)
    take = lambda count: [refs.pop(0) for _ in range(count)]
    weights, shards = take(mats), take(parts)
    carry_in = take(1)[0] if sums_in else None
    src = take(1)[0] if "sourced" in finish else None
    stage, osem, ssem = refs[-3:]
    keeps = not {"carry", "sourced"}.isdisjoint(finish)
    n_out = sum(f in ("emit", "send") for f in finish) + keeps
    outs = refs[-3 - n_out:-3]
    carry_out = outs.pop(0) if keeps else None
    rows, unknowns = weights[0].shape
    depth = unknowns // own.shape[1]
    height = rows // blocks
    if src is not None:
        src_in = pltpu.make_async_copy(src.at[0, tick], stage.at[0], ssem)
        src_in.start()
        src_in.wait()
    columns = [
        pl.ds(pl.multiple_of(own[0, places[i]] * depth + offsets[i], 128), shards[i].shape[0])
        for i in range(parts)]

    def block(r, carry):
        lines = pl.ds(pl.multiple_of(r * height, height), height)
        for m in range(mats):
            total = carry_in[first + m, lines, :] if sums_in else None
            for i in range(parts):
                product = jnp.dot(weights[m][lines, columns[i]], shards[i][...],
                                  preferred_element_type=jnp.float32)
                total = product if total is None else total + product
            if finish[m] == "sourced":
                total = total + stage[0, lines, :].astype(jnp.float32)
            if finish[m] in ("carry", "sourced"):
                carry_out[first + m, lines, :] = total
            elif finish[m] == "emit":
                stage[m, lines, :] = total.astype(stage.dtype)
            else:
                outs[m][lines, :] = total.astype(stage.dtype)
        return carry

    lax.fori_loop(0, blocks, block, 0)
    pending = [(stage.at[m], outs[m].at[0, tick]) for m in range(mats) if finish[m] == "emit"]
    pending = [pltpu.make_async_copy(a, b, osem.at[k]) for k, (a, b) in enumerate(pending)]
    for c in pending:
        c.start()
    for c in pending:
        c.wait()


def in_vmem(x):
    return pltpu.with_memory_space_constraint(x, pltpu.VMEM)


def in_hbm(x):
    return pltpu.with_memory_space_constraint(x, pltpu.HBM)


def accumulate(own, weights, parts, carry, first, finish, tick, sources, held):
    mats, (rows, unknowns) = len(weights), weights[0].shape
    cols = parts[0][0].shape[1]
    depth = sum(p[0].shape[0] for p in parts)
    args = [own, *[in_vmem(w) for w in weights], *[in_vmem(p[0]) for p in parts]]
    specs = [SMEM] + [VMEM] * (len(args) - 1)
    shapes, out_specs, aliases = [], [], {}
    if not {"carry", "sourced"}.isdisjoint(finish):
        shapes.append(jax.ShapeDtypeStruct((4, rows, cols), jnp.float32))
        out_specs.append(VMEM)
        if carry is not None:
            aliases[len(args)] = 0
    if carry is not None:
        args.append(in_vmem(carry))
        specs.append(VMEM)
    if "sourced" in finish:
        args.append(in_hbm(sources))
        specs.append(ANY)
    for m, f in enumerate(finish):
        if f == "emit":
            if held[m] is not None:
                aliases[len(args)] = len(shapes)
                args.append(in_hbm(held[m]))
                specs.append(ANY)
            shapes.append(jax.ShapeDtypeStruct((1, sources.shape[1], rows, cols), jnp.bfloat16))
            out_specs.append(ANY)
        elif f == "send":
            shapes.append(jax.ShapeDtypeStruct((rows, cols), jnp.bfloat16))
            out_specs.append(VMEM)
    stages = mats if "emit" in finish else 1
    return pl.pallas_call(
        functools.partial(
            accumulate_kernel, tuple(p[1] for p in parts), tuple(p[2] for p in parts),
            carry is not None, first, tuple(finish), tick, 2),
        out_shape=tuple(shapes),
        in_specs=specs,
        out_specs=tuple(out_specs),
        input_output_aliases=aliases,
        scratch_shapes=[
            pltpu.VMEM((stages, rows, cols), jnp.bfloat16),
            pltpu.SemaphoreType.DMA((mats + 1,)),
            pltpu.SemaphoreType.DMA,
        ],
        compiler_params=pltpu.CompilerParams(vmem_limit_bytes=(2 << 20) + stages * rows * cols * 2),
        cost_estimate=pl.CostEstimate(
            flops=2 * mats * rows * depth * 512, bytes_accessed=2 * mats * rows * depth,
            transcendentals=0),
    )(*args)


def load_kernel(own, *refs):
    mats = (len(refs) - 3) // 2
    weights, x, held, carry, sem = refs[:mats], refs[mats], refs[mats + 1:-2], refs[-2], refs[-1]
    depth = x.shape[0]
    copies = [pltpu.make_async_copy(weights[m], held[m], sem.at[m]) for m in range(mats)]
    copies[0].start()
    columns = pl.ds(pl.multiple_of(own[0, 0] * depth, 128), depth)
    for m in range(mats):
        if m + 1 < mats:
            copies[m + 1].start()
        copies[m].wait()
        carry[m] = jnp.dot(held[m][:, columns], x[...], preferred_element_type=jnp.float32)


def load(own, weights, x):
    mats, (rows, unknowns) = len(weights), weights[0].shape
    held = [jax.ShapeDtypeStruct(w.shape, w.dtype) for w in weights]
    res = pl.pallas_call(
        load_kernel,
        out_shape=(*held, jax.ShapeDtypeStruct((mats, rows, x.shape[1]), jnp.float32)),
        in_specs=[SMEM] + [ANY] * mats + [VMEM],
        out_specs=(VMEM,) * (mats + 1),
        scratch_shapes=[pltpu.SemaphoreType.DMA((mats,))],
        compiler_params=pltpu.CompilerParams(vmem_limit_bytes=2 << 20),
        cost_estimate=pl.CostEstimate(
            flops=2 * mats * rows * x.shape[0] * 512, bytes_accessed=4 * mats * rows * unknowns,
            transcendentals=0),
    )(own, *[in_hbm(w) for w in weights], in_vmem(x))
    return res[:mats], res[mats]


def sweep(layers, n, transmission, reflection, receiver_map, midplane_map, traces, sources):
    ticks = sources.shape[1]
    weights = [transmission[0], reflection[0], receiver_map[0], midplane_map[0]]
    own = lax.dynamic_slice_in_dim(jnp.asarray(owner_table(n)), lax.axis_index("row"), 1, 0)
    outs = [None] * 3
    incoming = traces[0]
    half = incoming.shape[0] // 2
    last_step = n // 2
    late = None

    def multiply(which, parts, carry, finish, tick, held=None):
        return accumulate(own, [weights[i] for i in which], parts, carry, which[0], finish, tick,
                          sources, held)

    for tick in range(ticks):
        final = tick + 1 == ticks
        up = down = incoming
        ready = [(incoming, 0, 0)]
        carry = None if tick == 0 else carry
        for s in range(1, last_step + 1):
            if s < last_step:
                new_up = ring_hop(up, n, 1)
                new_down = ring_hop(down, n, -1)
                arrived = [(new_up, 2 * s - 1, 0), (new_down, 2 * s, 0)]
            else:
                new_up = ring_hop(up[:half], n, 1)
                new_down = ring_hop(down[half:], n, -1)
                arrived = [(new_up, n - 1, 0), (new_down, n - 1, half)]
            if s == 1:
                if tick == 0:
                    weights, carry = load(own, weights, incoming)
                    ready = []
                else:
                    outs = list(multiply((1, 2, 3), late, carry, ["emit"] * 3, tick - 1, outs))
                    carry = None
            else:
                source = "sourced" if s == last_step else "carry"
                if s < last_step or final:
                    carry = multiply((0, 1, 2, 3), ready, carry, [source] + ["carry"] * 3, tick)[0]
                    late = []
                else:
                    carry = multiply((0,), ready, carry, [source], tick)[0]
                    late = ready
                ready = []
            ready = ready + arrived
            up, down = new_up, new_down
        if final:
            res = multiply((0, 1, 2, 3), ready, carry, ["send"] + ["emit"] * 3, tick,
                           [None] + outs)
            return res[1], res[2], res[3], res[0][None]
        sent = multiply((0,), ready, carry, ["send"], tick)[0]
        late = late + ready
        incoming = lax.ppermute(sent, "layer", [(i, i + 1) for i in range(layers - 1)])


def plain_program(layers, transmission, reflection, receiver_map, midplane_map, traces, sources):
    incoming = sent = traces[0]
    outs = [[], [], []]
    for tick in range(sources.shape[1]):
        piece = lax.all_gather(incoming, "row", axis=0, tiled=True)
        total = jnp.dot(transmission[0], piece, preferred_element_type=jnp.float32)
        sent = (total + sources[0, tick].astype(jnp.float32)).astype(jnp.bfloat16)
        for out, w in zip(outs, (reflection, receiver_map, midplane_map)):
            out.append(jnp.dot(w[0], piece, preferred_element_type=jnp.float32).astype(jnp.bfloat16))
        incoming = lax.ppermute(sent, "layer", [(i, i + 1) for i in range(layers - 1)])
    return tuple(jnp.stack(o)[None] for o in outs) + (sent[None],)


def solution(mesh):
    layers, n = mesh.shape["layer"], mesh.shape["row"]

    def body(transmission, reflection, receiver_map, midplane_map, traces, sources):
        args = (transmission, reflection, receiver_map, midplane_map, traces, sources)
        if traces.shape[1] % 256 or n % 2 or n < 4:
            return plain_program(layers, *args)
        return sweep(layers, n, *args)

    wide = P("layer", "row", None)
    deep = P("layer", None, "row", None)
    return jax.shard_map(
        body,
        mesh=mesh,
        in_specs=(wide, wide, wide, wide, wide, deep),
        out_specs=(deep, deep, deep, wide),
        check_vma=False,
    )
```

time: 272 us -> 232 us (0.85)
  the two profiles are of different devices: /device:TPU:0 before, /device:TPU:30 now
where the time goes in v2:
time: 232 us; the launch traced here: 231 us
  Pallas kernels  94.6 us (41%)
  waiting for transfers between devices  83.7 us (36%)
  starting transfers between devices  28.9 us (12%)
  local copies, waits for them, and re-layouts  22.5 us (10%)
    pallas_call x14, Pallas kernels, accumulate(): pl.pallas_call(functools.partial(accumulate_kernel, tuple((p[1] for p in...  81.3 us
    ppermute x24, waiting for transfers between devices, ring_hop(): lax.ppermute(x, 'row', [(order[i], order[(i + by) % n]) for i in range(n)])  65.3 us
    ppermute x24, starting transfers between devices, ring_hop(): lax.ppermute(x, 'row', [(order[i], order[(i + by) % n]) for i in range(n)])  24.7 us
    unnamed x70, local copies, waits for them, and re-layouts  21.6 us
    ppermute x2, waiting for transfers between devices, sweep(): lax.ppermute(sent, 'layer', [(i, i + 1) for i in range(layers - 1)])  18.4 us
    pallas_call x1, Pallas kernels, load(): pl.pallas_call(load_kernel, out_shape=(*held, jax.ShapeDtypeStruct((mats,...  13.3 us
  transfers between devices with their start and end apart: 26, of which 10 were waited for; matrix products, arithmetic and copies ran while one was open for 0% of the time, Pallas kernels for 37%

profile of v2, /device:TPU:30, one launch (start us, length us, event | category | flops | bytes accessed | tf_op | source)
XLA Modules:
  0.0 231.0 jit_solution(13607613259177532766)
XLA Ops:
  2.7 13.3 %collective-permute-done.refs_4_ = bf16[768,384]{1,0:T(8,128)(2,1)S(1)} collective-permute-done((bf16[768,384]{1,0:T(8,128)(2,1)}, bf16[768,384]{1,0:T(8,128)(2,1)S(1)}, u32[]{:S(2)}, u32[]{:S(2)}) %collective-permute-start) | collective-permute-done | bytes 589856 | tf_op jit(solution)/shard_map/ppermute | solution.py:34
  20.3 10.0 %collective-permute-done.1.refs_4_ = bf16[768,384]{1,0:T(8,128)(2,1)} collective-permute-done((bf16[768,384]{1,0:T(8,128)(2,1)S(1)}, bf16[768,384]{1,0:T(8,128)(2,1)}, u32[]{:S(2)}, u32[]{:S(2)}) %collective-permute-start.1) | collective-permute-done | bytes 589856 | tf_op jit(solution)/shard_map/ppermute | solution.py:34
  33.9 13.3 %shard_map.102 = (bf16[768,6144]{1,0:T(8,128)(2,1)S(1)}, bf16[768,6144]{1,0:T(8,128)(2,1)S(1)}, bf16[768,6144]{1,0:T(8,128)(2,1)S(1)}, bf16[768,6144]{1,0:T(8,128)(2,1)S(1)}, f32[4,768,384]{2,1,0:T(8,128)S(1)}) custom-call(s32[1,8]{1,0:T(1,128)S(1)} %constant_dynamic-slice_fusion.own, bf16[768,6144]{1,0:T(8,128)(2,1)} %bitcast.15, ...), custom_call_target="tpu_custom_call" | custom-call | flops 2415919104 | bytes 75497472 | tf_op jit(solution)/shard_map/pallas_call | solution.py:162
  47.2 6.2 %shard_map.103.refs_6_ = f32[4,768,384]{2,1,0:T(8,128)S(1)} custom-call(s32[1,8]{1,0:T(1,128)S(1)} %constant_dynamic-slice_fusion.own, bf16[768,6144]{1,0:T(8,128)(2,1)S(1)} %get-tuple-element.19.refs_0_, bf16[768,6144]{1,0:T(8,128)(2,1)S(1)} %get-tuple-element.20.refs_1_.refs_0_, ...), custom_call_target="tpu_custom_call", output_to_operand_aliasing={{}: (7, {})} | custom-call | flops 4831838208 | bytes 9437184 | tf_op jit(solution)/shard_map/pallas_call | solution.py:125
  55.6 3.7 %copy-done.1 = bf16[768,6144]{1,0:T(8,128)(2,1)S(1)} copy-done((bf16[768,6144]{1,0:T(8,128)(2,1)S(1)}, bf16[768,6144]{1,0:T(8,128)(2,1)}, u32[]{:S(2)}) %copy-start.1) | copy-done | bytes 9437208
  59.3 6.9 %shard_map.104.refs_3_ = f32[4,768,384]{2,1,0:T(8,128)S(1)} custom-call(s32[1,8]{1,0:T(1,128)S(1)} %constant_dynamic-slice_fusion.own, bf16[768,6144]{1,0:T(8,128)(2,1)S(1)} %get-tuple-element.19.refs_0_, bf16[768,6144]{1,0:T(8,128)(2,1)S(1)} %get-tuple-element.20.refs_1_.refs_0_, bf16[768,6144]{1,0:T(8,128)(2,1)S(1)} %copy-done.1, ...), custom_call_target="tpu_custom_call", output_to_operand_aliasing={{}: (7, {})} | custom-call | flops 4831838208 | bytes 9437184 | tf_op jit(solution)/shard_map/pallas_call | solution.py:125
  66.3 3.5 %shard_map.105.refs_3_.refs_7_ = f32[4,768,384]{2,1,0:T(8,128)S(1)} custom-call(s32[1,8]{1,0:T(1,128)S(1)} %constant_dynamic-slice_fusion.own, bf16[768,6144]{1,0:T(8,128)(2,1)S(1)} %get-tuple-element.19.refs_0_, bf16[768,384]{1,0:T(8,128)(2,1)S(1)} %collective-permute-done.2.refs_1_.refs_3_, ...), custom_call_target="tpu_custom_call", output_to_operand_aliasing={{}: (4, {})} | custom-call | flops 1207959552 | bytes 2359296 | tf_op jit(solution)/shard_map/pallas_call | solution.py:125
  73.8 9.1 %collective-permute-done.8.refs_4_ = bf16[768,384]{1,0:T(8,128)(2,1)S(1)} collective-permute-done((bf16[768,384]{1,0:T(8,128)(2,1)S(1)}, bf16[768,384]{1,0:T(8,128)(2,1)S(1)}, u32[]{:S(2)}, u32[]{:S(2)}) %collective-permute-start.8) | collective-permute-done | bytes 589856 | tf_op jit(solution)/shard_map/ppermute | solution.py:228
  85.0 13.6 %collective-permute-done.9.refs_5_ = bf16[768,384]{1,0:T(8,128)(2,1)S(1)} collective-permute-done((bf16[768,384]{1,0:T(8,128)(2,1)S(1)}, bf16[768,384]{1,0:T(8,128)(2,1)S(1)}, u32[]{:S(2)}, u32[]{:S(2)}) %collective-permute-start.9) | collective-permute-done | bytes 589856 | tf_op jit(solution)/shard_map/ppermute | solution.py:34
  100.9 13.7 %collective-permute-done.10.refs_4_ = bf16[768,384]{1,0:T(8,128)(2,1)S(1)} collective-permute-done((bf16[768,384]{1,0:T(8,128)(2,1)S(1)}, bf16[768,384]{1,0:T(8,128)(2,1)S(1)}, u32[]{:S(2)}, u32[]{:S(2)}) %collective-permute-start.10) | collective-permute-done | bytes 589856 | tf_op jit(solution)/shard_map/ppermute | solution.py:34
  116.6 8.3 %shard_map.107.refs_6_ = f32[4,768,384]{2,1,0:T(8,128)S(1)} custom-call(s32[1,8]{1,0:T(1,128)S(1)} %constant_dynamic-slice_fusion.own, bf16[768,6144]{1,0:T(8,128)(2,1)S(1)} %get-tuple-element.19.refs_0_, bf16[768,6144]{1,0:T(8,128)(2,1)S(1)} %get-tuple-element.20.refs_1_.refs_0_, bf16[768,6144]{1,0:T(8,128)(2,1)S(1)} %copy-done.1, ...), custom_call_target="tpu_custom_call" | custom-call | flops 7247757312 | bytes 14155776 | tf_op jit(solution)/shard_map/pallas_call | solution.py:125
  130.0 2.3 %copy-done.6 = f32[4,768,384]{2,1,0:T(8,128)S(1)} copy-done((f32[4,768,384]{2,1,0:T(8,128)S(1)}, f32[4,768,384]{2,1,0:T(8,128)}, u32[]{:S(2)}) %copy-start.6) | copy-done | bytes 4718616
  134.5 6.1 %shard_map.108.refs_3_ = f32[4,768,384]{2,1,0:T(8,128)S(1)} custom-call(s32[1,8]{1,0:T(1,128)S(1)} %constant_dynamic-slice_fusion.own, bf16[768,6144]{1,0:T(8,128)(2,1)S(1)} %get-tuple-element.19.refs_0_, bf16[768,6144]{1,0:T(8,128)(2,1)S(1)} %get-tuple-element.20.refs_1_.refs_0_, bf16[768,6144]{1,0:T(8,128)(2,1)S(1)} %bitcast.7, ...), custom_call_target="tpu_custom_call", output_to_operand_aliasing={{}: (7, {})} | custom-call | flops 4831838208 | bytes 9437184 | tf_op jit(solution)/shard_map/pallas_call | solution.py:125
  140.6 3.2 %shard_map.109.refs_3_.refs_7_ = f32[4,768,384]{2,1,0:T(8,128)S(1)} custom-call(s32[1,8]{1,0:T(1,128)S(1)} %constant_dynamic-slice_fusion.own, bf16[768,6144]{1,0:T(8,128)(2,1)S(1)} %get-tuple-element.19.refs_0_, bf16[768,384]{1,0:T(8,128)(2,1)S(1)} %copy-done.10, bf16[768,384]{1,0:T(8,128)(2,1)S(1)} %copy-done.12, ...), custom_call_target="tpu_custom_call", output_to_operand_aliasing={{}: (4, {})} | custom-call | flops 1207959552 | bytes 2359296 | tf_op jit(solution)/shard_map/pallas_call | solution.py:125
  147.9 9.3 %collective-permute-done.17.refs_4_ = bf16[768,384]{1,0:T(8,128)(2,1)S(1)} collective-permute-done((bf16[768,384]{1,0:T(8,128)(2,1)S(1)}, bf16[768,384]{1,0:T(8,128)(2,1)S(1)}, u32[]{:S(2)}, u32[]{:S(2)}) %collective-permute-start.17) | collective-permute-done | bytes 589856 | tf_op jit(solution)/shard_map/ppermute | solution.py:228
  159.2 13.7 %collective-permute-done.18.refs_5_ = bf16[768,384]{1,0:T(8,128)(2,1)S(1)} collective-permute-done((bf16[768,384]{1,0:T(8,128)(2,1)S(1)}, bf16[768,384]{1,0:T(8,128)(2,1)S(1)}, u32[]{:S(2)}, u32[]{:S(2)}) %collective-permute-start.18) | collective-permute-done | bytes 589856 | tf_op jit(solution)/shard_map/ppermute | solution.py:34
  175.2 3.7 %copy-done.2 = bf16[768,6144]{1,0:T(8,128)(2,1)S(1)} copy-done((bf16[768,6144]{1,0:T(8,128)(2,1)S(1)}, bf16[768,6144]{1,0:T(8,128)(2,1)}, u32[]{:S(2)}) %copy-start.2) | copy-done | bytes 9437208
  178.9 8.1 %shard_map.114 = (bf16[1,3,768,384]{3,2,1,0:T(8,128)(2,1)}, bf16[1,3,768,384]{3,2,1,0:T(8,128)(2,1)}, bf16[1,3,768,384]{3,2,1,0:T(8,128)(2,1)}) custom-call(s32[1,8]{1,0:T(1,128)S(1)} %constant_dynamic-slice_fusion.own, bf16[768,6144]{1,0:T(8,128)(2,1)S(1)} %get-tuple-element.20.refs_1_.refs_0_, bf16[768,6144]{1,0:T(8,128)(2,1)S(1)} %copy-done.2, ...), custom_call_target="tpu_custom_call" | custom-call | flops 5435817984 | bytes 10616832 | tf_op jit(solution)/shard_map/pallas_call | solution.py:125
  187.0 8.1 %shard_map.115 = (bf16[1,3,768,384]{3,2,1,0:T(8,128)(2,1)}, bf16[1,3,768,384]{3,2,1,0:T(8,128)(2,1)}, bf16[1,3,768,384]{3,2,1,0:T(8,128)(2,1)}) custom-call(s32[1,8]{1,0:T(1,128)S(1)} %constant_dynamic-slice_fusion.own, bf16[768,6144]{1,0:T(8,128)(2,1)S(1)} %get-tuple-element.20.refs_1_.refs_0_, ...), custom_call_target="tpu_custom_call", output_to_operand_aliasing={{0}: (9, {}), {1}: (10, {}), {2}: (11, {})} | custom-call | flops 5435817984 | bytes 10616832 | tf_op jit(solution)/shard_map/pallas_call | solution.py:125
  197.2 8.3 %shard_map.111.refs_6_ = f32[4,768,384]{2,1,0:T(8,128)S(1)} custom-call(s32[1,8]{1,0:T(1,128)S(1)} %constant_dynamic-slice_fusion.own, bf16[768,6144]{1,0:T(8,128)(2,1)S(1)} %get-tuple-element.19.refs_0_, bf16[768,6144]{1,0:T(8,128)(2,1)S(1)} %get-tuple-element.20.refs_1_.refs_0_, bf16[768,6144]{1,0:T(8,128)(2,1)S(1)} %copy-done.2, ...), custom_call_target="tpu_custom_call" | custom-call | flops 7247757312 | bytes 14155776 | tf_op jit(solution)/shard_map/pallas_call | solution.py:125
  205.6 3.7 %copy-done.4 = bf16[768,6144]{1,0:T(8,128)(2,1)S(1)} copy-done((bf16[768,6144]{1,0:T(8,128)(2,1)S(1)}, bf16[768,6144]{1,0:T(8,128)(2,1)}, u32[]{:S(2)}) %copy-start.4) | copy-done | bytes 9437208
  209.2 6.1 %shard_map.112.refs_6_ = f32[4,768,384]{2,1,0:T(8,128)S(1)} custom-call(s32[1,8]{1,0:T(1,128)S(1)} %constant_dynamic-slice_fusion.own, bf16[768,6144]{1,0:T(8,128)(2,1)S(1)} %get-tuple-element.19.refs_0_, bf16[768,6144]{1,0:T(8,128)(2,1)S(1)} %get-tuple-element.20.refs_1_.refs_0_, bf16[768,6144]{1,0:T(8,128)(2,1)S(1)} %copy-done.2, ...), custom_call_target="tpu_custom_call", output_to_operand_aliasing={{}: (7, {})} | custom-call | flops 4831838208 | bytes 9437184 | tf_op jit(solution)/shard_map/pallas_call | solution.py:125
  217.6 7.2 %shard_map.113.refs_6_ = f32[4,768,384]{2,1,0:T(8,128)S(1)} custom-call(s32[1,8]{1,0:T(1,128)S(1)} %constant_dynamic-slice_fusion.own, bf16[768,6144]{1,0:T(8,128)(2,1)S(1)} %get-tuple-element.19.refs_0_, bf16[768,6144]{1,0:T(8,128)(2,1)S(1)} %get-tuple-element.20.refs_1_.refs_0_, bf16[768,6144]{1,0:T(8,128)(2,1)S(1)} %bitcast.9, ...), custom_call_target="tpu_custom_call", output_to_operand_aliasing={{}: (7, {})} | custom-call | flops 4831838208 | bytes 9437184 | tf_op jit(solution)/shard_map/pallas_call | solution.py:125
  224.9 5.9 %shard_map.116 = (bf16[768,384]{1,0:T(8,128)(2,1)}, bf16[1,3,768,384]{3,2,1,0:T(8,128)(2,1)}, bf16[1,3,768,384]{3,2,1,0:T(8,128)(2,1)}, bf16[1,3,768,384]{3,2,1,0:T(8,128)(2,1)}) custom-call(s32[1,8]{1,0:T(1,128)S(1)} %constant_dynamic-slice_fusion.own, ...), custom_call_target="tpu_custom_call", output_to_operand_aliasing={{1}: (8, {}), {2}: (9, {}), {3}: (10, {})} | custom-call | flops 2415919104 | bytes 4718592 | tf_op jit(solution)/shard_map/pallas_call | solution.py:125
  (123 shorter events, 42.4 us)
Async XLA Ops:
  0.6 15.3 %collective-permute-start = (bf16[768,384]{1,0:T(8,128)(2,1)}, bf16[768,384]{1,0:T(8,128)(2,1)S(1)}, u32[]{:S(2)}, u32[]{:S(2)}) collective-permute-start(bf16[768,384]{1,0:T(8,128)(2,1)} %bitcast.12), channel_id=1, source_target_pairs={{0,2},{2,4},{4,6},{6,7},{7,5},{5,3},{3,1},{1,0},{8,10},{10,12},{12... | collective-permute-start | bytes 1769480 | tf_op jit(solution)/shard_map/ppermute | solution.py:34
  1.1 16.1 %collective-permute-start.4 = (bf16[768,384]{1,0:T(8,128)(2,1)}, bf16[768,384]{1,0:T(8,128)(2,1)S(1)}, u32[]{:S(2)}, u32[]{:S(2)}) collective-permute-start(bf16[768,384]{1,0:T(8,128)(2,1)} %bitcast.13), channel_id=1, source_target_pairs={{0,1},{2,0},{4,2},{6,4},{7,6},{5,7},{3,5},{1,3},{8,9},{10,8},{12,1... | collective-permute-start | bytes 1769480 | tf_op jit(solution)/shard_map/ppermute | solution.py:34
  16.0 14.3 %collective-permute-start.1 = (bf16[768,384]{1,0:T(8,128)(2,1)S(1)}, bf16[768,384]{1,0:T(8,128)(2,1)}, u32[]{:S(2)}, u32[]{:S(2)}) collective-permute-start(bf16[768,384]{1,0:T(8,128)(2,1)S(1)} %collective-permute-done.refs_4_), channel_id=1, source_target_pairs={{0,2},{2,4},{4,6},{6,7},{7,5},{5,3},{3,1},{1,0},{8,10},{10,12},{12... | collective-permute-start | bytes 1769480 | tf_op jit(solution)/shard_map/ppermute | solution.py:34
  17.2 14.0 %collective-permute-start.5 = (bf16[768,384]{1,0:T(8,128)(2,1)S(1)}, bf16[768,384]{1,0:T(8,128)(2,1)}, u32[]{:S(2)}, u32[]{:S(2)}) collective-permute-start(bf16[768,384]{1,0:T(8,128)(2,1)S(1)} %collective-permute-done.4.refs_5_), channel_id=1, source_target_pairs={{0,1},{2,0},{4,2},{6,4},{7,6},{5,7},{3,5},{1,3},{8,9},{10,8},{12,1... | collective-permute-start | bytes 1769480 | tf_op jit(solution)/shard_map/ppermute | solution.py:34
  30.3 23.1 %collective-permute-start.2 = (bf16[768,384]{1,0:T(8,128)(2,1)}, bf16[768,384]{1,0:T(8,128)(2,1)S(1)}, u32[]{:S(2)}, u32[]{:S(2)}) collective-permute-start(bf16[768,384]{1,0:T(8,128)(2,1)} %collective-permute-done.1.refs_4_), channel_id=1, source_target_pairs={{0,2},{2,4},{4,6},{6,7},{7,5},{5,3},{3,1},{1,0},{8,10},{10,12},{12... | collective-permute-start | bytes 1769480 | tf_op jit(solution)/shard_map/ppermute | solution.py:34
  31.3 22.7 %collective-permute-start.6 = (bf16[768,384]{1,0:T(8,128)(2,1)}, bf16[768,384]{1,0:T(8,128)(2,1)S(1)}, u32[]{:S(2)}, u32[]{:S(2)}) collective-permute-start(bf16[768,384]{1,0:T(8,128)(2,1)} %collective-permute-done.5.refs_5_), channel_id=1, source_target_pairs={{0,1},{2,0},{4,2},{6,4},{7,6},{5,7},{3,5},{1,3},{8,9},{10,8},{12,1... | collective-permute-start | bytes 1769480 | tf_op jit(solution)/shard_map/ppermute | solution.py:34
  53.5 16.3 %collective-permute-start.3 = (bf16[384,384]{1,0:T(8,128)(2,1)S(1)}, bf16[384,384]{1,0:T(8,128)(2,1)S(1)}, u32[]{:S(2)}, u32[]{:S(2)}) collective-permute-start(bf16[384,384]{1,0:T(8,128)(2,1)S(1)} %slice.24), channel_id=1, source_target_pairs={{0,2},{2,4},{4,6},{6,7},{7,5},{5,3},{3,1},{1,0},{8,10},{10,12},{12... | collective-permute-start | bytes 884744 | tf_op jit(solution)/shard_map/ppermute | solution.py:34
  54.0 15.8 %collective-permute-start.7 = (bf16[384,384]{1,0:T(8,128)(2,1)S(1)}, bf16[384,384]{1,0:T(8,128)(2,1)S(1)}, u32[]{:S(2)}, u32[]{:S(2)}) collective-permute-start(bf16[384,384]{1,0:T(8,128)(2,1)S(1)} %slice.25), channel_id=1, source_target_pairs={{0,1},{2,0},{4,2},{6,4},{7,6},{5,7},{3,5},{1,3},{8,9},{10,8},{12,1... | collective-permute-start | bytes 884744 | tf_op jit(solution)/shard_map/ppermute | solution.py:34
  71.5 11.5 %collective-permute-start.8 = (bf16[768,384]{1,0:T(8,128)(2,1)S(1)}, bf16[768,384]{1,0:T(8,128)(2,1)S(1)}, u32[]{:S(2)}, u32[]{:S(2)}) collective-permute-start(bf16[768,384]{1,0:T(8,128)(2,1)S(1)} %shard_map.106), channel_id=1, source_target_pairs={{0,8},{8,16},{16,24},{1,9},{9,17},{17,25},{2,10},{10,18},{18,26},{... | collective-permute-start | bytes 1769480 | tf_op jit(solution)/shard_map/ppermute | solution.py:228
  83.0 15.6 %collective-permute-start.9 = (bf16[768,384]{1,0:T(8,128)(2,1)S(1)}, bf16[768,384]{1,0:T(8,128)(2,1)S(1)}, u32[]{:S(2)}, u32[]{:S(2)}) collective-permute-start(bf16[768,384]{1,0:T(8,128)(2,1)S(1)} %collective-permute-done.8.refs_4_), channel_id=1, source_target_pairs={{0,2},{2,4},{4,6},{6,7},{7,5},{5,3},{3,1},{1,0},{8,10},{10,12},{12... | collective-permute-start | bytes 1769480 | tf_op jit(solution)/shard_map/ppermute | solution.py:34
  83.3 15.9 %collective-permute-start.13 = (bf16[768,384]{1,0:T(8,128)(2,1)S(1)}, bf16[768,384]{1,0:T(8,128)(2,1)S(1)}, u32[]{:S(2)}, u32[]{:S(2)}) collective-permute-start(bf16[768,384]{1,0:T(8,128)(2,1)S(1)} %collective-permute-done.8.refs_4_), channel_id=1, source_target_pairs={{0,1},{2,0},{4,2},{6,4},{7,6},{5,7},{3,5},{1,3},{8,9},{10,8},{12,1... | collective-permute-start | bytes 1769480 | tf_op jit(solution)/shard_map/ppermute | solution.py:34
  98.6 16.0 %collective-permute-start.10 = (bf16[768,384]{1,0:T(8,128)(2,1)S(1)}, bf16[768,384]{1,0:T(8,128)(2,1)S(1)}, u32[]{:S(2)}, u32[]{:S(2)}) collective-permute-start(bf16[768,384]{1,0:T(8,128)(2,1)S(1)} %collective-permute-done.9.refs_5_), channel_id=1, source_target_pairs={{0,2},{2,4},{4,6},{6,7},{7,5},{5,3},{3,1},{1,0},{8,10},{10,12},{12... | collective-permute-start | bytes 1769480 | tf_op jit(solution)/shard_map/ppermute | solution.py:34
  99.2 15.7 %collective-permute-start.14 = (bf16[768,384]{1,0:T(8,128)(2,1)S(1)}, bf16[768,384]{1,0:T(8,128)(2,1)S(1)}, u32[]{:S(2)}, u32[]{:S(2)}) collective-permute-start(bf16[768,384]{1,0:T(8,128)(2,1)S(1)} %collective-permute-done.13.refs_6_), channel_id=1, source_target_pairs={{0,1},{2,0},{4,2},{6,4},{7,6},{5,7},{3,5},{1,3},{8,9},{10,8},{12,1... | collective-permute-start | bytes 1769480 | tf_op jit(solution)/shard_map/ppermute | solution.py:34
  114.5 12.5 %collective-permute-start.11 = (bf16[768,384]{1,0:T(8,128)(2,1)S(1)}, bf16[768,384]{1,0:T(8,128)(2,1)S(1)}, u32[]{:S(2)}, u32[]{:S(2)}) collective-permute-start(bf16[768,384]{1,0:T(8,128)(2,1)S(1)} %collective-permute-done.10.refs_4_), channel_id=1, source_target_pairs={{0,2},{2,4},{4,6},{6,7},{7,5},{5,3},{3,1},{1,0},{8,10},{10,12},{12... | collective-permute-start | bytes 1769480 | tf_op jit(solution)/shard_map/ppermute | solution.py:34
  114.9 12.6 %collective-permute-start.15 = (bf16[768,384]{1,0:T(8,128)(2,1)S(1)}, bf16[768,384]{1,0:T(8,128)(2,1)S(1)}, u32[]{:S(2)}, u32[]{:S(2)}) collective-permute-start(bf16[768,384]{1,0:T(8,128)(2,1)S(1)} %collective-permute-done.14.refs_5_), channel_id=1, source_target_pairs={{0,1},{2,0},{4,2},{6,4},{7,6},{5,7},{3,5},{1,3},{8,9},{10,8},{12,1... | collective-permute-start | bytes 1769480 | tf_op jit(solution)/shard_map/ppermute | solution.py:34
  127.1 16.8 %collective-permute-start.12 = (bf16[384,384]{1,0:T(8,128)(2,1)S(1)}, bf16[384,384]{1,0:T(8,128)(2,1)S(1)}, u32[]{:S(2)}, u32[]{:S(2)}) collective-permute-start(bf16[384,384]{1,0:T(8,128)(2,1)S(1)} %slice.26), channel_id=1, source_target_pairs={{0,2},{2,4},{4,6},{6,7},{7,5},{5,3},{3,1},{1,0},{8,10},{10,12},{12... | collective-permute-start | bytes 884744 | tf_op jit(solution)/shard_map/ppermute | solution.py:34
  128.3 15.6 %collective-permute-start.16 = (bf16[384,384]{1,0:T(8,128)(2,1)S(1)}, bf16[384,384]{1,0:T(8,128)(2,1)S(1)}, u32[]{:S(2)}, u32[]{:S(2)}) collective-permute-start(bf16[384,384]{1,0:T(8,128)(2,1)S(1)} %slice.27), channel_id=1, source_target_pairs={{0,1},{2,0},{4,2},{6,4},{7,6},{5,7},{3,5},{1,3},{8,9},{10,8},{12,1... | collective-permute-start | bytes 884744 | tf_op jit(solution)/shard_map/ppermute | solution.py:34
  145.9 11.2 %collective-permute-start.17 = (bf16[768,384]{1,0:T(8,128)(2,1)S(1)}, bf16[768,384]{1,0:T(8,128)(2,1)S(1)}, u32[]{:S(2)}, u32[]{:S(2)}) collective-permute-start(bf16[768,384]{1,0:T(8,128)(2,1)S(1)} %shard_map.110), channel_id=1, source_target_pairs={{0,8},{8,16},{16,24},{1,9},{9,17},{17,25},{2,10},{10,18},{18,26},{... | collective-permute-start | bytes 1769480 | tf_op jit(solution)/shard_map/ppermute | solution.py:228
  157.1 15.7 %collective-permute-start.18 = (bf16[768,384]{1,0:T(8,128)(2,1)S(1)}, bf16[768,384]{1,0:T(8,128)(2,1)S(1)}, u32[]{:S(2)}, u32[]{:S(2)}) collective-permute-start(bf16[768,384]{1,0:T(8,128)(2,1)S(1)} %collective-permute-done.17.refs_4_), channel_id=1, source_target_pairs={{0,2},{2,4},{4,6},{6,7},{7,5},{5,3},{3,1},{1,0},{8,10},{10,12},{12... | collective-permute-start | bytes 1769480 | tf_op jit(solution)/shard_map/ppermute | solution.py:34
  157.5 16.0 %collective-permute-start.22 = (bf16[768,384]{1,0:T(8,128)(2,1)S(1)}, bf16[768,384]{1,0:T(8,128)(2,1)S(1)}, u32[]{:S(2)}, u32[]{:S(2)}) collective-permute-start(bf16[768,384]{1,0:T(8,128)(2,1)S(1)} %collective-permute-done.17.refs_4_), channel_id=1, source_target_pairs={{0,1},{2,0},{4,2},{6,4},{7,6},{5,7},{3,5},{1,3},{8,9},{10,8},{12,1... | collective-permute-start | bytes 1769480 | tf_op jit(solution)/shard_map/ppermute | solution.py:34
  172.9 22.3 %collective-permute-start.19 = (bf16[768,384]{1,0:T(8,128)(2,1)S(1)}, bf16[768,384]{1,0:T(8,128)(2,1)S(1)}, u32[]{:S(2)}, u32[]{:S(2)}) collective-permute-start(bf16[768,384]{1,0:T(8,128)(2,1)S(1)} %collective-permute-done.18.refs_5_), channel_id=1, source_target_pairs={{0,2},{2,4},{4,6},{6,7},{7,5},{5,3},{3,1},{1,0},{8,10},{10,12},{12... | collective-permute-start | bytes 1769480 | tf_op jit(solution)/shard_map/ppermute | solution.py:34
  173.5 22.0 %collective-permute-start.23 = (bf16[768,384]{1,0:T(8,128)(2,1)S(1)}, bf16[768,384]{1,0:T(8,128)(2,1)S(1)}, u32[]{:S(2)}, u32[]{:S(2)}) collective-permute-start(bf16[768,384]{1,0:T(8,128)(2,1)S(1)} %collective-permute-done.22.refs_6_), channel_id=1, source_target_pairs={{0,1},{2,0},{4,2},{6,4},{7,6},{5,7},{3,5},{1,3},{8,9},{10,8},{12,1... | collective-permute-start | bytes 1769480 | tf_op jit(solution)/shard_map/ppermute | solution.py:34
  195.1 20.3 %collective-permute-start.20 = (bf16[768,384]{1,0:T(8,128)(2,1)S(1)}, bf16[768,384]{1,0:T(8,128)(2,1)S(1)}, u32[]{:S(2)}, u32[]{:S(2)}) collective-permute-start(bf16[768,384]{1,0:T(8,128)(2,1)S(1)} %collective-permute-done.19.refs_4_), channel_id=1, source_target_pairs={{0,2},{2,4},{4,6},{6,7},{7,5},{5,3},{3,1},{1,0},{8,10},{10,12},{12... | collective-permute-start | bytes 1769480 | tf_op jit(solution)/shard_map/ppermute | solution.py:34
  195.5 20.3 %collective-permute-start.24 = (bf16[768,384]{1,0:T(8,128)(2,1)S(1)}, bf16[768,384]{1,0:T(8,128)(2,1)S(1)}, u32[]{:S(2)}, u32[]{:S(2)}) collective-permute-start(bf16[768,384]{1,0:T(8,128)(2,1)S(1)} %collective-permute-done.23.refs_5_), channel_id=1, source_target_pairs={{0,1},{2,0},{4,2},{6,4},{7,6},{5,7},{3,5},{1,3},{8,9},{10,8},{12,1... | collective-permute-start | bytes 1769480 | tf_op jit(solution)/shard_map/ppermute | solution.py:34
  (37 other events, 564.3 us)
